TPU v7x, 32 devices: a whole 2x2x4 slice. The times are simulated.
32 devices in a mesh: groups: 2 (over y), cable: 4 (over z), bins: 2 (over x), pairs: 2 (over core).
Axes of the slice: x: 2, y: 2, z: 4, core: 2. Of those that a mesh axis runs over, the one named last changes fastest.
Arguments:
- spectra: bfloat16 [4, 16, 256, 2048], P('groups', None, 'cable', 'bins'), parts along dimension 0, may hold values from -6 to 6
- counts: int32 [8], P(('groups', 'cable')), parts along dimension 0, may hold values from 1 to 4, as said below
- owners: int32 [8, 4], P(('groups', 'cable')), parts along dimension 0, may hold values from 0 to 1
Outputs:
- stacks: float32 [4, 4, 320, 2048], P('groups', 'cable', 'pairs', 'bins'), parts along dimension 0
There are 2 independent parts, one for each index of `groups`. A program takes and returns all parts, laid end to end along the dimension named above; each array names one. Nothing has to cross between parts.
Inputs may be any that keep to these rules, and one draw needn't show every extreme that they name: `counts`: block 0 keeps 4 offsets and block 1 keeps 1.
All inputs are finite; a program needn't handle non-finite values.
Results may differ from a plain program's by a relative error of at most 0.0017.
Values may be sent and summed in bfloat16 or wider, within the bound.
A program may use at most 128 MiB of HBM per device.

v0:
```python
import math

import jax
import jax.numpy as jnp
import numpy as np
from jax import lax
from jax.experimental import pallas as pl
from jax.experimental.pallas import tpu as pltpu
from jax.sharding import PartitionSpec as P

REACH = 3
HALF_WIDTH = 32


epsilon = 1e-06
band_rows = 16


def with_halo(x, sides, width):
    for axis, dim in sides:
        count, length = (lax.axis_size(axis), x.shape[dim])
        up = [(i, (i + 1) % count) for i in range(count - 1)]
        down = [(j, i) for i, j in up]
        last = lax.slice_in_dim(x, length - width, length, axis=dim)
        first = lax.slice_in_dim(x, 0, width, axis=dim)
        before = lax.ppermute(last, axis, up)
        after = lax.ppermute(first, axis, down)
        x = jnp.concatenate([before, x, after], axis=dim)
    return x


def from_behind(block, axis, distance):
    devices = range(lax.axis_size(axis))
    route = [(i - distance, i) for i in devices if i - distance in devices]
    return lax.ppermute(block, axis, route)


def whiten_rows(spectra):
    real_part = spectra[0].astype(jnp.float32)
    imag_part = spectra[1].astype(jnp.float32)
    power_sum = real_part * real_part + imag_part * imag_part
    padded = with_halo(power_sum, (("bins", 2),), HALF_WIDTH)
    window_len = 2 * HALF_WIDTH + 1
    window_sum = lax.reduce_window(
        padded, jnp.zeros((), padded.dtype), lax.add, (1, 1, window_len), (1, 1, 1), "VALID"
    )
    inverse_amp = lax.rsqrt(window_sum / window_len + epsilon)
    return jnp.stack(
        [
            (real_part * inverse_amp).astype(jnp.bfloat16),
            (imag_part * inverse_amp).astype(jnp.bfloat16),
        ]
    )


def make_lag_table(col_count):
    flattened = jnp.arange(band_rows * col_count)
    row_of = flattened // col_count
    col_of = flattened % col_count
    lag_lanes = jnp.arange(col_count + band_rows - 1)
    return (lag_lanes[None, :] == (col_of - row_of + band_rows - 1)[:, None]).astype(jnp.bfloat16)


def lag_stack(pair_block, lag_table):
    freq_count, row_count, col_count = pair_block.shape
    group_count = row_count // band_rows
    grouped = pair_block.reshape(freq_count, group_count, band_rows * col_count)
    banded = jnp.einsum("fgk,ku->fgu", grouped, lag_table, preferred_element_type=jnp.float32)
    lag_sums = jnp.zeros((freq_count, col_count + row_count - 1), jnp.float32)
    for row_group in range(group_count):
        first_lag = row_count - band_rows * (row_group + 1)
        lag_sums = lag_sums.at[:, first_lag : first_lag + col_count + band_rows - 1].add(
            banded[:, row_group]
        )
    return lag_sums.T


def correlate(left_rows, right_rows, factor, lag_table):
    left_real = jnp.concatenate([left_rows[0], left_rows[1]], axis=0)
    left_imag = jnp.concatenate([left_rows[1], -left_rows[0]], axis=0)
    right_both = jnp.concatenate([right_rows[0], right_rows[1]], axis=0)
    corr_real = (
        jnp.einsum("wif,wjf->fij", left_real, right_both, preferred_element_type=jnp.float32)
        * factor
    ).astype(jnp.bfloat16)
    corr_imag = (
        jnp.einsum("wif,wjf->fij", left_imag, right_both, preferred_element_type=jnp.float32)
        * factor
    ).astype(jnp.bfloat16)
    return jnp.stack([lag_stack(corr_real, lag_table), lag_stack(corr_imag, lag_table)])


def general_shards(spectra, counts, owners):
    pair_devs = lax.axis_size("pairs")
    member = lax.axis_index("pairs")
    channels = spectra.shape[2]
    half_rows = channels // pair_devs
    source = whiten_rows(spectra)
    receiver = lax.dynamic_slice_in_dim(source, member * half_rows, half_rows, 2)
    block_count = lax.axis_size("cable")
    cable_index = lax.axis_index("cable")
    live_count = jnp.minimum(counts[0], block_count - cable_index)
    panels = {0: receiver}
    for offset in range(1, REACH + 1):
        panels[offset] = from_behind(receiver, "cable", -offset)
    factor = 1.0 / math.sqrt(source.shape[1] * channels)
    lag_table = make_lag_table(half_rows)
    freq_count = source.shape[3]
    stacks = jnp.zeros((2, (REACH + 2) * channels, freq_count), jnp.float32)
    for offset in range(REACH + 1):
        lag_piece = correlate(source, panels[offset], factor, lag_table)
        weight = (offset < live_count).astype(jnp.float32)
        if offset == 0:
            kept_here = weight * lag_piece
        else:
            sent_away = owners[0, offset].astype(jnp.float32)
            arrived = from_behind(weight * sent_away * lag_piece, "cable", offset)
            kept_here = weight * (1.0 - sent_away) * lag_piece + arrived
        first_lag = offset * channels + member * half_rows
        current = lax.dynamic_slice_in_dim(stacks, first_lag, kept_here.shape[1], 1)
        stacks = lax.dynamic_update_slice_in_dim(stacks, current + kept_here, first_lag, 1)
    summed = lax.psum_scatter(stacks, "pairs", scatter_dimension=1, tiled=True)
    return summed[:, None]


EDGE = 128
BAND = 128
GROUP = 2
EARLY = 3
F32 = jnp.float32
MESH = pl.DeviceIdType.MESH


def channel_transforms(channels, factor):
    points = 2 * channels
    index = np.arange(points)
    angle = 2 * np.pi * np.outer(index, np.arange(channels)) / points
    cos, sin = np.cos(angle), np.sin(angle)
    full = np.block([[cos, sin], [-sin, cos]])
    high = full.astype(jnp.bfloat16)
    low = (full - high.astype(np.float64)).astype(jnp.bfloat16)
    forward = np.concatenate([high, low], axis=1)
    angle = 2 * np.pi * np.outer(index - (channels - 1), index) / points
    cos, sin = np.cos(angle), np.sin(angle)
    cos[-1], sin[-1] = 0.0, 0.0
    inverse = np.block([[cos, sin], [-sin, cos]]) * (factor / points)
    return jnp.asarray(forward), jnp.asarray(inverse.astype(np.float32))


def smoothing_window():
    distance = np.arange(BAND + 2 * EDGE)[:, None] - (np.arange(BAND)[None, :] + EDGE)
    ones = (np.abs(distance) <= HALF_WIDTH).astype(jnp.bfloat16)
    return jnp.asarray(np.concatenate([ones, ones], axis=0))


def stack_kernel(
    spectra_ref, counts_ref, owners_ref, window_ref, forward_ref, inverse_ref, out_ref,
    x_ref, flag_ref, white, far, back, spec, other, third, sums, sums_back, sums_far, stack, near_out, piece_back, near_in, arrived, swapped, seen,
    chain_send, chain_recv, back_send, back_recv, piece_send, piece_recv,
    next_send, next_recv, swap_send, swap_recv, flag_send, flag_recv, load_sem, edge_send, edge_recv,
):
    windows, channels = x_ref.shape[1:3]
    half = x_ref.shape[3] - 2 * EDGE
    bands, groups = half // BAND, windows // GROUP
    points = 2 * channels
    kept = out_ref.shape[1]
    blocks, halves = lax.axis_size("cable"), lax.axis_size("pairs")
    z, m = lax.axis_index("cable"), lax.axis_index("pairs")
    cuts, x = lax.axis_size("bins"), lax.axis_index("bins")
    bins = spectra_ref.shape[3]
    first = m == 0
    mirrored = jnp.where((x > 0) & (first | (x == cuts - 1)), 1, 0)
    onward = {"cable": lax.rem(z + 1, blocks)}
    backward = {"cable": lax.rem(z + blocks - 1, blocks)}
    partner = {"pairs": lax.rem(m + 1, halves)}

    def remote(source, target, send, recv, device):
        return pltpu.make_async_remote_copy(
            src_ref=source, dst_ref=target, send_sem=send, recv_sem=recv, device_id=device, device_id_type=MESH
        )

    def first_hop(s):
        return remote(white.at[s], far.at[s], chain_send.at[s], chain_recv.at[s], onward)

    def next_hop(s):
        return remote(far.at[s], far.at[s], chain_send.at[s], chain_recv.at[s], onward)

    def back_hop(s):
        return remote(white.at[s], back.at[s], back_send.at[s], back_recv.at[s], backward)

    def near_rows(source, target):
        begin, end = source * channels, source * channels + points + (source - 1) * channels
        return begin, max(begin, target * kept), min(end, (target + 1) * kept)

    def to_first(c, source, target, sender, spot_of):
        begin, low, high = near_rows(source, target)
        return remote(
            near_out.at[c, :, low - begin : high - begin],
            near_in.at[source - 1, sender, spot_of, :, low - target * kept : high - target * kept],
            piece_send.at[target, c],
            piece_recv.at[source - 1, sender, spot_of],
            {"cable": 0, "pairs": target},
        )

    def to_next(c):
        return remote(piece_back.at[c], arrived.at[c], next_send.at[c], next_recv.at[c], onward)

    def swap(c):
        rows = pl.ds(pl.multiple_of((1 - m) * kept, 8), kept)
        return remote(
            stack.at[c, :, rows], swapped.at[place(c)], swap_send.at[c], swap_recv.at[place(c)], partner
        )

    def place(c):
        return c + mirrored * (bands - 1 - 2 * c)

    def load(q):
        near = pl.multiple_of(m * (half - EDGE), EDGE)
        spot = pl.multiple_of((1 - m) * EDGE, EDGE)
        rows = pl.ds(q * GROUP, GROUP)
        return pltpu.make_async_copy(
            spectra_ref.at[:, rows, :, pl.ds(near, half + EDGE)],
            x_ref.at[:, rows, :, pl.ds(spot, half + EDGE)],
            load_sem.at[q],
        )

    spot = pl.ds(pl.multiple_of(m * (half + EDGE), EDGE), EDGE)

    def edge():
        source = pl.ds(pl.multiple_of((1 - m) * (bins - EDGE), EDGE), EDGE)
        target = {"bins": lax.rem(x + cuts + 1 - 2 * m, cuts)}
        return remote(
            spectra_ref.at[:, :, :, source], x_ref.at[:, :, :, spot], edge_send.at[0], edge_recv.at[0], target
        )

    def flags_to(block):
        return remote(flag_ref, seen, flag_send.at[block - 1], flag_recv.at[0], {"cable": block})

    for q in range(groups):
        load(q).start()
    live = jnp.minimum(counts_ref[0], blocks - z)
    for offset in range(REACH + 1):
        flag_ref[offset : offset + 1, :] = jnp.full((1, BAND), owners_ref[0, offset].astype(F32))
        weight = jnp.where(offset < live, 1.0, 0.0)
        flag_ref[REACH + 1 + offset : REACH + 2 + offset, :] = jnp.full((1, BAND), weight)
    barrier = pltpu.get_barrier_semaphore()
    for step in range(1, blocks):
        pl.semaphore_signal(barrier, inc=1, device_id={"cable": lax.rem(z + step, blocks)}, device_id_type=MESH)
        across = {"cable": lax.rem(z + step, blocks), "pairs": lax.rem(m + 1, halves)}
        pl.semaphore_signal(barrier, inc=1, device_id=across, device_id_type=MESH)
    pl.semaphore_signal(barrier, inc=1, device_id=partner, device_id_type=MESH)
    for step in range(1, cuts):
        pl.semaphore_signal(barrier, inc=1, device_id={"bins": lax.rem(x + step, cuts)}, device_id_type=MESH)
    pl.semaphore_wait(barrier, 2 * blocks + cuts - 2)
    sends_edge = (first & (x < cuts - 1)) | (~first & (x > 0))
    takes_edge = (first & (x > 0)) | (~first & (x < cuts - 1))

    @pl.when(sends_edge)
    def _():
        edge().start()

    @pl.when(~takes_edge)
    def _():
        x_ref[:, :, :, spot] = jnp.zeros((2, windows, channels, EDGE), x_ref.dtype)


    @pl.when(z == 0)
    def _():
        for block in range(1, blocks - 1):
            flags_to(block).start()

    def whiten(q, begin, count, store):
        lanes = pl.ds(pl.multiple_of(begin, BAND), count * BAND + 2 * EDGE)
        reals, imags, highs, lows = [], [], [], []
        for i in range(GROUP):
            real = x_ref[0, q * GROUP + i, :, lanes].astype(F32)
            imag = x_ref[1, q * GROUP + i, :, lanes].astype(F32)
            power = real * real + imag * imag
            high = power.astype(jnp.bfloat16)
            reals.append(real)
            imags.append(imag)
            highs.append(high)
            lows.append((power - high.astype(F32)).astype(jnp.bfloat16))
        high = jnp.concatenate(highs, axis=0)
        low = jnp.concatenate(lows, axis=0)
        for j in range(count):
            reach = slice(j * BAND, (j + 1) * BAND + 2 * EDGE)
            terms = jnp.concatenate([high[:, reach], low[:, reach]], axis=1)
            total = jnp.dot(terms, window_ref[...], preferred_element_type=F32)
            gain = lax.rsqrt(total / (2 * HALF_WIDTH + 1) + epsilon)
            here = slice(EDGE + j * BAND, EDGE + (j + 1) * BAND)
            slot = store(j) * groups + q
            for i in range(GROUP):
                rows = gain[i * channels : (i + 1) * channels]
                white[slot, i, :channels] = (reals[i][:, here] * rows).astype(jnp.bfloat16)
                white[slot, i, channels:] = (imags[i][:, here] * rows).astype(jnp.bfloat16)

    def whiten_inner(q, carry):
        load(q).wait()
        whiten(q, mirrored * BAND, bands - 1, lambda j: j + mirrored * (bands - 2 - 2 * j))

        @pl.when(z == 0)
        def _():
            first_hop(q).start()

        @pl.when(z == blocks - 1)
        def _():
            back_hop(q).start()

        return carry

    def whiten_last(q, carry):
        whiten(q, (1 - mirrored) * (bands - 1) * BAND, 1, lambda j: bands - 1)
        s = (bands - 1) * groups + q

        @pl.when(z == 0)
        def _():
            first_hop(s).start()

        @pl.when(z == blocks - 1)
        def _():
            back_hop(s).start()

        return carry

    def relay(s):
        next_hop(s).wait_recv()
        next_hop(s).start()

    def relay_early(s, count):
        @pl.when(z == 1)
        def _():
            for k in range(count):
                relay(s + k)

    lax.fori_loop(0, groups, whiten_inner, 0)
    relay_early(0, 1)

    @pl.when(z == 0)
    def _():
        @pl.loop(groups, (bands - 1) * groups)
        def _(s):
            first_hop(s).start()

    @pl.when(z == blocks - 1)
    def _():
        @pl.loop(groups, (bands - 1) * groups)
        def _(s):
            back_hop(s).start()

    @pl.when(takes_edge)
    def _():
        edge().wait_recv()

    lax.fori_loop(0, groups, whiten_last, 0)
    relay_early(1, 2)

    def transform(buffer, s):
        wide = jnp.concatenate([buffer[s, i] for i in range(GROUP)], axis=1)
        return jnp.dot(forward_ref[...], jnp.concatenate([wide, wide], axis=0), preferred_element_type=F32)

    tile = 32

    def power_into(total, s):
        for k in range(0, points, tile):
            gained = total[k : k + tile]
            for i in range(GROUP):
                lanes = slice(i * BAND, (i + 1) * BAND)
                real = spec[s, k : k + tile, lanes]
                imag = spec[s, points + k : points + k + tile, lanes]
                gained = gained + (real * real + imag * imag)
            total[k : k + tile] = gained

    def cross_into(total, near, far):
        for k in range(0, points, tile):
            gained_real = total[k : k + tile]
            gained_imag = total[points + k : points + k + tile]
            for i in range(GROUP):
                lanes = slice(i * BAND, (i + 1) * BAND)
                near_real = near[k : k + tile, lanes]
                near_imag = near[points + k : points + k + tile, lanes]
                far_real = far[k : k + tile, lanes]
                far_imag = far[points + k : points + k + tile, lanes]
                gained_real = gained_real + (near_real * far_real + near_imag * far_imag)
                gained_imag = gained_imag + (near_imag * far_real - near_real * far_imag)
            total[k : k + tile] = gained_real
            total[points + k : points + k + tile] = gained_imag

    def lags_of(values, columns):
        return jnp.dot(
            inverse_ref[:, :columns], values, preferred_element_type=F32, precision=lax.Precision.HIGHEST
        )

    def add_piece(c, first, piece):
        rows = pl.ds(first, points)
        stack[c, 0, rows] += piece[:points]
        stack[c, 1, rows] += piece[points:]

    def own_band(c, carry):
        sums[...] = jnp.zeros_like(sums)

        def step(q, inner):
            s = c * groups + q
            spec[s] = transform(white, s)
            power_into(sums, s)
            return inner

        lax.fori_loop(0, groups, step, 0)
        stack[c] = jnp.zeros(stack.shape[1:], F32)
        add_piece(c, 0, flag_ref[REACH + 1 : REACH + 2, :] * lags_of(sums[:points], points))
        relay_early(EARLY + c, 1)
        return carry

    lax.fori_loop(0, bands, own_band, 0)

    def counted_far(offset):
        return seen[offset : offset + 1, :] * seen[REACH + 1 + offset : REACH + 2 + offset, :]

    def counted_near(offset):
        return (1.0 - seen[offset : offset + 1, :]) * seen[REACH + 1 + offset : REACH + 2 + offset, :]

    @pl.when(z == 1)
    def _():
        flags_to(1).wait_recv()

        def band(c, carry):
            sums[...] = jnp.zeros_like(sums)

            def step(q, inner):
                s = c * groups + q

                @pl.when(s >= EARLY + bands)
                def _():
                    relay(s)

                other[...] = transform(far, s)
                cross_into(sums, other, spec.at[s])
                return inner

            lax.fori_loop(0, groups, step, 0)
            piece = lags_of(sums[...], 2 * points)
            near = (counted_near(1) * piece).astype(near_out.dtype)
            near_out[c, 0, :points] = near[:points]
            near_out[c, 1, :points] = near[points:]
            for target in range(2):
                to_first(c, 1, target, m, place(c)).start()
            add_piece(c, channels, counted_far(1) * piece)
            swap(c).start()
            return carry

        lax.fori_loop(0, bands, band, 0)

    @pl.when(z == 2)
    def _():
        flags_to(1).wait_recv()

        def band(c, carry):
            sums[...] = jnp.zeros_like(sums)
            sums_back[...] = jnp.zeros_like(sums_back)
            sums_far[...] = jnp.zeros_like(sums_far)

            def step(q, inner):
                s = c * groups + q
                back_hop(s).wait_recv()
                third[...] = transform(back, s)
                cross_into(sums_back, spec.at[s], third)

                @pl.when(q == groups - 1)
                def _():
                    sums_back[...] = flag_ref[REACH + 2 : REACH + 3, :] * lags_of(sums_back[...], 2 * points)

                next_hop(s).wait_recv()
                other[...] = transform(far, s)
                cross_into(sums, other, spec.at[s])
                cross_into(sums_far, other, third)
                return inner

            lax.fori_loop(0, groups, step, 0)
            both = lags_of(jnp.concatenate([sums[...], sums_far[...]], axis=1), 2 * points)
            piece, distant = both[:, :BAND], both[:, BAND:]
            near, beyond = counted_near(2) * piece, counted_near(3) * distant
            for part in range(2):
                top = part * points
                shared = near[top + channels : top + points] + beyond[top : top + channels]
                near_out[c, part, :channels] = near[top : top + channels].astype(near_out.dtype)
                near_out[c, part, channels:points] = shared.astype(near_out.dtype)
                near_out[c, part, points:] = beyond[top + channels : top + points].astype(near_out.dtype)
            for target in range(2):
                to_first(c, 2, target, m, place(c)).start()
            ahead = sums_back[...]
            sent = flag_ref[1:2, :]
            piece_back[c, 0] = (sent * ahead).astype(piece_back.dtype)
            piece_back[c, 1] = (counted_far(3) * distant).astype(piece_back.dtype)
            to_next(c).start()
            add_piece(c, 2 * channels, counted_far(2) * piece)
            add_piece(c, channels, (1.0 - sent) * ahead)
            swap(c).start()
            return carry

        lax.fori_loop(0, bands, band, 0)

    @pl.when(z == blocks - 1)
    def _():
        def band(c, carry):
            to_next(c).wait_recv()
            add_piece(c, channels, arrived[c, 0].astype(F32))
            add_piece(c, 3 * channels, arrived[c, 1].astype(F32))
            swap(c).start()
            return carry

        lax.fori_loop(0, bands, band, 0)

    @pl.when(z == 0)
    def _():
        @pl.loop(0, bands)
        def _(c):
            swap(c).start()

    def collect(c, carry):
        mine = pl.ds(pl.multiple_of(m * half + place(c) * BAND, BAND), BAND)
        theirs = pl.ds(pl.multiple_of((1 - m) * half + place(c) * BAND, BAND), BAND)
        out_ref[:, :, mine] = stack[c, :, pl.ds(pl.multiple_of(m * kept, 8), kept)]
        swap(c).wait_recv()
        out_ref[:, :, theirs] = swapped[place(c)]
        swap(c).wait_send()
        return carry

    lax.fori_loop(0, bands, collect, 0)

    def add_near(target):
        def band(c, carry):
            for source in range(1, 3):
                _, low, high = near_rows(source, target)
                rows = slice(low - target * kept, high - target * kept)
                for sender in range(2):
                    to_first(c, source, target, sender, place(c)).wait_recv()
                    lanes = pl.ds(pl.multiple_of(sender * half + place(c) * BAND, BAND), BAND)
                    out_ref[:, rows, lanes] += near_in[source - 1, sender, place(c), :, rows].astype(F32)
            return carry

        lax.fori_loop(0, bands, band, 0)

    @pl.when((z == 0) & (m == 0))
    def _():
        add_near(0)

    @pl.when((z == 0) & (m == 1))
    def _():
        add_near(1)

    @pl.when(sends_edge)
    def _():
        edge().wait_send()

    @pl.when(z < 2)
    def _():
        @pl.loop(0, bands * groups)
        def _(s):
            next_hop(s).wait_send()

    @pl.when(z == blocks - 1)
    def _():
        @pl.loop(0, bands * groups)
        def _(s):
            back_hop(s).wait_send()

    @pl.when(z == 1)
    def _():
        @pl.loop(0, bands)
        def _(c):
            for target in range(2):
                to_first(c, 1, target, m, place(c)).wait_send()

    @pl.when(z == 2)
    def _():
        @pl.loop(0, bands)
        def _(c):
            for target in range(2):
                to_first(c, 2, target, m, place(c)).wait_send()
            to_next(c).wait_send()

    @pl.when(z == 0)
    def _():
        for block in range(1, blocks - 1):
            flags_to(block).wait_send()


def four_block_shards(spectra, counts, owners):
    parts, windows, channels, bins = spectra.shape
    halves, blocks = lax.axis_size("pairs"), lax.axis_size("cable")
    half, points = bins // halves, 2 * channels
    forward, inverse = channel_transforms(channels, 1.0 / math.sqrt(windows * channels))
    bands, groups = half // BAND, windows // GROUP
    pieces = bands * groups
    rows = (REACH + 2) * channels
    kept = rows // halves
    block = pltpu.VMEM((pieces, GROUP, points, BAND), jnp.bfloat16)
    spectrum = pltpu.VMEM((2 * points, GROUP * BAND), F32)
    sums = pltpu.VMEM((2 * points, BAND), F32)

    def lags(lead):
        return pltpu.VMEM(lead + (2 * points, BAND), jnp.bfloat16)

    dma = pltpu.SemaphoreType.DMA
    out = pl.pallas_call(
        stack_kernel,
        out_shape=jax.ShapeDtypeStruct((2, kept, bins), F32),
        in_specs=[
            pl.BlockSpec(memory_space=pl.ANY),
            pl.BlockSpec(memory_space=pltpu.SMEM),
            pl.BlockSpec(memory_space=pltpu.SMEM),
            pl.BlockSpec(memory_space=pltpu.VMEM),
            pl.BlockSpec(memory_space=pltpu.VMEM),
            pl.BlockSpec(memory_space=pltpu.VMEM),
        ],
        out_specs=pl.BlockSpec(memory_space=pltpu.VMEM),
        scratch_shapes=[
            pltpu.VMEM((2, windows, channels, half + 2 * EDGE), jnp.bfloat16),
            pltpu.VMEM((2 * (REACH + 1), BAND), F32),
            block, block, block,
            pltpu.VMEM((pieces, 2 * points, GROUP * BAND), F32),
            spectrum, spectrum, sums, sums, sums,
            pltpu.VMEM((bands, 2, rows, BAND), F32),
            pltpu.VMEM((bands, 2, points + channels, BAND), jnp.bfloat16),
            lags((bands, 2)),
            pltpu.VMEM((2, halves, bands, 2, kept, BAND), jnp.bfloat16),
            lags((bands, 2)),
            pltpu.VMEM((bands, 2, kept, BAND), F32),
            pltpu.VMEM((2 * (REACH + 1), BAND), F32),
            dma((pieces,)), dma((pieces,)), dma((pieces,)), dma((pieces,)),
            dma((halves, bands)), dma((2, halves, bands)),
            dma((bands,)), dma((bands,)), dma((bands,)), dma((bands,)),
            dma((blocks - 1,)), dma((1,)),
            dma((groups,)), dma((1,)), dma((1,)),
        ],
        compiler_params=pltpu.CompilerParams(
            collective_id=0, has_side_effects=True, vmem_limit_bytes=60 * 1024 * 1024
        ),
    )(spectra, counts, owners, smoothing_window(), forward, inverse)
    return out[:, None]


def solution(mesh):
    sizes = dict(mesh.shape)
    fits = sizes["cable"] == REACH + 1 and sizes["pairs"] == 2
    shards = four_block_shards if fits else general_shards
    placed = (
        P("groups", None, "cable", "bins"),
        P(("groups", "cable")),
        P(("groups", "cable"), None),
    )
    return jax.shard_map(
        shards,
        mesh=mesh,
        in_specs=placed,
        out_specs=P("groups", "cable", "pairs", "bins"),
        check_vma=False,
    )
```

profile of v0, /device:TPU:1, one launch (start us, length us, event | category | flops | bytes accessed | tf_op | source)
XLA Modules:
  0.0 70.6 jit_solution(15562942195469875880)
XLA Ops:
  0.7 67.4 %shard_map.64 = f32[2,160,1024]{2,1,0:T(8,128)} custom-call(bf16[2,16,64,1024]{3,2,1,0:T(8,128)(2,1)} %spectra_ref.1, s32[1]{0:T(128)S(6)} %copy.9.counts_ref, s32[1,4]{1,0:T(1,128)} %owners_ref.1, bf16[768,128]{1,0:T(8,128)(2,1)} %constant.8.clone.window_ref, bf16[256,256]{1,0:T(8,128)(2,1)} %constant.6.clone.forward_ref, f32[256,256]{1,0:T(8,128)} %constant.7.clone.inverse_ref), custom_call_target="tpu_custom_call" | custom-call | tf_op jit(solution)/shard_map/pallas_call | solution.py:605
  68.0 2.5 %copy.10 = f32[2,1,160,1024]{3,2,1,0:T(8,128)} copy(f32[2,1,160,1024]{3,2,1,0:T(8,128)} %bitcast.3) | data formatting | bytes 2621440
where the time goes:
time: 70.7 us; the launch traced here: 70.6 us
  Pallas kernels  67.4 us (95%)
  local copies, waits for them, and re-layouts  2.52 us (4%)
    pallas_call x1, Pallas kernels, four_block_shards(): pl.pallas_call(stack_kernel, out_shape=jax.ShapeDtypeStruct((2, kept, bin...  67.4 us
    unnamed x1, local copies, waits for them, and re-layouts  2.52 us

commit v1 on v0

v1 whole, which is shorter than its diff:
```python
import math

import jax
import jax.numpy as jnp
import numpy as np
from jax import lax
from jax.experimental import pallas as pl
from jax.experimental.pallas import tpu as pltpu
from jax.sharding import PartitionSpec as P

REACH = 3
HALF_WIDTH = 32


epsilon = 1e-06
band_rows = 16


def with_halo(x, sides, width):
    for axis, dim in sides:
        count, length = (lax.axis_size(axis), x.shape[dim])
        up = [(i, (i + 1) % count) for i in range(count - 1)]
        down = [(j, i) for i, j in up]
        last = lax.slice_in_dim(x, length - width, length, axis=dim)
        first = lax.slice_in_dim(x, 0, width, axis=dim)
        before = lax.ppermute(last, axis, up)
        after = lax.ppermute(first, axis, down)
        x = jnp.concatenate([before, x, after], axis=dim)
    return x


def from_behind(block, axis, distance):
    devices = range(lax.axis_size(axis))
    route = [(i - distance, i) for i in devices if i - distance in devices]
    return lax.ppermute(block, axis, route)


def whiten_rows(spectra):
    real_part = spectra[0].astype(jnp.float32)
    imag_part = spectra[1].astype(jnp.float32)
    power_sum = real_part * real_part + imag_part * imag_part
    padded = with_halo(power_sum, (("bins", 2),), HALF_WIDTH)
    window_len = 2 * HALF_WIDTH + 1
    window_sum = lax.reduce_window(
        padded, jnp.zeros((), padded.dtype), lax.add, (1, 1, window_len), (1, 1, 1), "VALID"
    )
    inverse_amp = lax.rsqrt(window_sum / window_len + epsilon)
    return jnp.stack(
        [
            (real_part * inverse_amp).astype(jnp.bfloat16),
            (imag_part * inverse_amp).astype(jnp.bfloat16),
        ]
    )


def make_lag_table(col_count):
    flattened = jnp.arange(band_rows * col_count)
    row_of = flattened // col_count
    col_of = flattened % col_count
    lag_lanes = jnp.arange(col_count + band_rows - 1)
    return (lag_lanes[None, :] == (col_of - row_of + band_rows - 1)[:, None]).astype(jnp.bfloat16)


def lag_stack(pair_block, lag_table):
    freq_count, row_count, col_count = pair_block.shape
    group_count = row_count // band_rows
    grouped = pair_block.reshape(freq_count, group_count, band_rows * col_count)
    banded = jnp.einsum("fgk,ku->fgu", grouped, lag_table, preferred_element_type=jnp.float32)
    lag_sums = jnp.zeros((freq_count, col_count + row_count - 1), jnp.float32)
    for row_group in range(group_count):
        first_lag = row_count - band_rows * (row_group + 1)
        lag_sums = lag_sums.at[:, first_lag : first_lag + col_count + band_rows - 1].add(
            banded[:, row_group]
        )
    return lag_sums.T


def correlate(left_rows, right_rows, factor, lag_table):
    left_real = jnp.concatenate([left_rows[0], left_rows[1]], axis=0)
    left_imag = jnp.concatenate([left_rows[1], -left_rows[0]], axis=0)
    right_both = jnp.concatenate([right_rows[0], right_rows[1]], axis=0)
    corr_real = (
        jnp.einsum("wif,wjf->fij", left_real, right_both, preferred_element_type=jnp.float32)
        * factor
    ).astype(jnp.bfloat16)
    corr_imag = (
        jnp.einsum("wif,wjf->fij", left_imag, right_both, preferred_element_type=jnp.float32)
        * factor
    ).astype(jnp.bfloat16)
    return jnp.stack([lag_stack(corr_real, lag_table), lag_stack(corr_imag, lag_table)])


def general_shards(spectra, counts, owners):
    pair_devs = lax.axis_size("pairs")
    member = lax.axis_index("pairs")
    channels = spectra.shape[2]
    half_rows = channels // pair_devs
    source = whiten_rows(spectra)
    receiver = lax.dynamic_slice_in_dim(source, member * half_rows, half_rows, 2)
    block_count = lax.axis_size("cable")
    cable_index = lax.axis_index("cable")
    live_count = jnp.minimum(counts[0], block_count - cable_index)
    panels = {0: receiver}
    for offset in range(1, REACH + 1):
        panels[offset] = from_behind(receiver, "cable", -offset)
    factor = 1.0 / math.sqrt(source.shape[1] * channels)
    lag_table = make_lag_table(half_rows)
    freq_count = source.shape[3]
    stacks = jnp.zeros((2, (REACH + 2) * channels, freq_count), jnp.float32)
    for offset in range(REACH + 1):
        lag_piece = correlate(source, panels[offset], factor, lag_table)
        weight = (offset < live_count).astype(jnp.float32)
        if offset == 0:
            kept_here = weight * lag_piece
        else:
            sent_away = owners[0, offset].astype(jnp.float32)
            arrived = from_behind(weight * sent_away * lag_piece, "cable", offset)
            kept_here = weight * (1.0 - sent_away) * lag_piece + arrived
        first_lag = offset * channels + member * half_rows
        current = lax.dynamic_slice_in_dim(stacks, first_lag, kept_here.shape[1], 1)
        stacks = lax.dynamic_update_slice_in_dim(stacks, current + kept_here, first_lag, 1)
    summed = lax.psum_scatter(stacks, "pairs", scatter_dimension=1, tiled=True)
    return summed[:, None]


EDGE = 128
BAND = 128
GROUP = 2
EARLY = 9
TABLE_ROWS = 2048
F32 = jnp.float32
BF16 = jnp.bfloat16
MESH = pl.DeviceIdType.MESH


def channel_transforms(channels, factor):
    points = 2 * channels
    index = np.arange(points)
    angle = 2 * np.pi * np.outer(index, np.arange(channels)) / points
    cos, sin = np.cos(angle), np.sin(angle)
    forward = split_high_low(np.block([[cos, sin], [-sin, cos]]))
    angle = 2 * np.pi * np.outer(index - (channels - 1), index) / points
    cos, sin = np.cos(angle), np.sin(angle)
    cos[-1], sin[-1] = 0.0, 0.0
    inverse = split_high_low(np.block([[cos, sin], [-sin, cos]]) * (factor / points))
    return forward, inverse


def split_high_low(full):
    high = full.astype(jnp.bfloat16)
    low = (full - high.astype(np.float64)).astype(jnp.bfloat16)
    return np.concatenate([high, low], axis=1)


def smoothing_window():
    distance = np.arange(BAND + 2 * EDGE)[:, None] - (np.arange(BAND)[None, :] + EDGE)
    ones = (np.abs(distance) <= HALF_WIDTH).astype(jnp.bfloat16)
    return np.concatenate([ones, ones], axis=0)


def stack_kernel(
    spectra_ref, counts_ref, owners_ref, tables_ref, out_ref,
    x_ref, window_ref, forward_ref, inverse_ref, flag_ref, seen,
    white, white0, white1, white2, white3, spec, one, two, three, sums_a, sums_b, sums_c,
    stack, near_out, far_out, inbox, swapped,
    load_sem, constant_sem, edge_send, edge_recv, flag_send, flag_recv,
    block_send, block_recv, result_send, result_recv, swap_send, swap_recv,
):
    windows, channels = x_ref.shape[1:3]
    half = x_ref.shape[3] - 2 * EDGE
    bands, groups = half // BAND, windows // GROUP
    pieces = bands * groups
    points = 2 * channels
    kept = out_ref.shape[1]
    blocks, halves = lax.axis_size("cable"), lax.axis_size("pairs")
    z, m = lax.axis_index("cable"), lax.axis_index("pairs")
    cuts, x = lax.axis_size("bins"), lax.axis_index("bins")
    bins = spectra_ref.shape[3]
    first = m == 0
    second = m == 1
    mirrored = x
    partner = {"pairs": 1 - m}

    def remote(source, target, send, recv, device):
        return pltpu.make_async_remote_copy(
            src_ref=source, dst_ref=target, send_sem=send, recv_sem=recv, device_id=device, device_id_type=MESH
        )

    received = (white0, white1, white2, white3)

    def own_to(block, s, lane, device):
        return remote(
            white.at[s], received[block].at[s], block_send.at[lane, s], block_recv.at[block, s], {"cable": device}
        )

    def pass_on(s, lane, device):
        return remote(
            white0.at[s], white0.at[s], block_send.at[lane, s], block_recv.at[0, s], {"cable": device}
        )

    def arrived(block, s):
        own_to(block, s, 0, 0).wait_recv()

    def sent(s, lane):
        own_to(0, s, lane, 0).wait_send()

    def place(c):
        return c + mirrored * (bands - 1 - 2 * c)

    def results(c, source, sender, buffer, begin, low, high, device, lane):
        copies = {}
        for target in range(halves):
            top, end = max(low, target * kept), min(high, (target + 1) * kept)
            if top < end:
                copies[target] = remote(
                    buffer.at[c, :, top - begin : end - begin],
                    inbox.at[source, sender, c, :, top - target * kept : end - target * kept],
                    result_send.at[lane, target, c],
                    result_recv.at[source, sender, c],
                    {"cable": device, "pairs": target},
                )
        return copies

    def start_all(copies):
        for copy in copies.values():
            copy.start()

    def finish_all(copies):
        for copy in copies.values():
            copy.wait_send()

    one_pair = channels + points
    two_pairs = 2 * channels + points
    three_pairs = 3 * channels + points

    def near_from_1(c, sender=m):
        return results(c, 1, sender, near_out, channels, channels, one_pair, 0, 0)

    def near_from_1_all(c, sender=m):
        return results(c, 1, sender, near_out, channels, channels, three_pairs, 0, 0)

    def near_from_2(c, sender=m):
        return results(c, 2, sender, near_out, 2 * channels, 2 * channels, three_pairs, 0, 0)

    def near_from_3(c, sender=m):
        return results(c, 3, sender, near_out, channels, 3 * channels, three_pairs, 0, 0)

    def near_pair_23(c, sender=m):
        return results(c, 3, sender, far_out, channels, channels, one_pair, 2, 1)

    def far_from_2(c, sender=m):
        return results(c, 2, sender, far_out, channels, channels, three_pairs, 3, 1)

    def far_pair_01(c, source, sender=m):
        return results(c, source, sender, near_out, channels, channels, one_pair, 1, 0)

    def far_pair_02(c, source, sender=m):
        return results(c, source, sender, far_out, 2 * channels, 2 * channels, two_pairs, 2, 1)

    def far_pair_03(c, source, sender=m):
        return results(c, source, sender, far_out, channels, 3 * channels, three_pairs, 3, 2)

    def swap(c):
        rows = pl.ds(pl.multiple_of((1 - m) * kept, 8), kept)
        return remote(stack.at[c, :, rows], swapped.at[c], swap_send.at[c], swap_recv.at[c], partner)

    def load(q):
        near = pl.multiple_of(m * (half - EDGE), EDGE)
        begin = pl.multiple_of((1 - m) * EDGE, EDGE)
        rows = pl.ds(q * GROUP, GROUP)
        return pltpu.make_async_copy(
            spectra_ref.at[:, rows, :, pl.ds(near, half + EDGE)],
            x_ref.at[:, rows, :, pl.ds(begin, half + EDGE)],
            load_sem.at[q],
        )

    constants, top = [], 0
    for i, table in enumerate((window_ref, forward_ref, inverse_ref)):
        rows, columns = table.shape
        source = tables_ref.at[top : top + rows, :columns]
        constants.append(pltpu.make_async_copy(source, table, constant_sem.at[i]))
        top += rows

    edge_lanes = pl.ds(pl.multiple_of(m * (half + EDGE), EDGE), EDGE)

    def edge():
        source = pl.ds(pl.multiple_of((1 - m) * (bins - EDGE), EDGE), EDGE)
        return remote(
            spectra_ref.at[:, :, :, source],
            x_ref.at[:, :, :, edge_lanes],
            edge_send.at[0],
            edge_recv.at[0],
            {"bins": 1 - x},
        )

    def flags_to(source, device, lane):
        return remote(
            flag_ref, seen.at[source], flag_send.at[lane], flag_recv.at[source], {"cable": device}
        )

    load(0).start()
    constants[0].start()
    for q in range(1, groups):
        load(q).start()
    constants[1].start()
    constants[2].start()
    live = jnp.minimum(counts_ref[0], blocks - z)
    for offset in range(REACH + 1):
        flag_ref[offset : offset + 1, :] = jnp.full((1, BAND), owners_ref[0, offset].astype(F32))
        weight = jnp.where(offset < live, 1.0, 0.0)
        flag_ref[REACH + 1 + offset : REACH + 2 + offset, :] = jnp.full((1, BAND), weight)
    barrier = pltpu.get_barrier_semaphore()
    for step in range(1, blocks):
        pl.semaphore_signal(barrier, inc=1, device_id={"cable": lax.rem(z + step, blocks)}, device_id_type=MESH)
        across = {"cable": lax.rem(z + step, blocks), "pairs": 1 - m}
        pl.semaphore_signal(barrier, inc=1, device_id=across, device_id_type=MESH)
    pl.semaphore_signal(barrier, inc=1, device_id=partner, device_id_type=MESH)
    pl.semaphore_signal(barrier, inc=1, device_id={"bins": 1 - x}, device_id_type=MESH)
    sends_edge = x == m
    takes_edge = x != m

    def whiten(q, begin, count, store):
        lanes = pl.ds(pl.multiple_of(begin, BAND), count * BAND + 2 * EDGE)
        reals, imags, highs, lows = [], [], [], []
        for i in range(GROUP):
            real = x_ref[0, q * GROUP + i, :, lanes].astype(F32)
            imag = x_ref[1, q * GROUP + i, :, lanes].astype(F32)
            power = real * real + imag * imag
            high = power.astype(BF16)
            reals.append(real)
            imags.append(imag)
            highs.append(high)
            lows.append((power - high.astype(F32)).astype(BF16))
        high = jnp.concatenate(highs, axis=0)
        low = jnp.concatenate(lows, axis=0)
        for j in range(count):
            reach = slice(j * BAND, (j + 1) * BAND + 2 * EDGE)
            terms = jnp.concatenate([high[:, reach], low[:, reach]], axis=1)
            total = jnp.dot(terms, window_ref[...], preferred_element_type=F32)
            gain = lax.rsqrt(total / (2 * HALF_WIDTH + 1) + epsilon)
            here = slice(EDGE + j * BAND, EDGE + (j + 1) * BAND)
            slot = store(j) * groups + q
            for i in range(GROUP):
                rows = gain[i * channels : (i + 1) * channels]
                white[slot, i, :channels] = (reals[i][:, here] * rows).astype(BF16)
                white[slot, i, channels:] = (imags[i][:, here] * rows).astype(BF16)

    def whiten_inner(q):
        load(q).wait()
        whiten(q, mirrored * BAND, bands - 1, lambda j: j + mirrored * (bands - 2 - 2 * j))

    def send_inner(q):
        @pl.when(z == 0)
        def _():
            own_to(0, q + groups * m, 0, 1).start()

        @pl.when((z == 1) & second)
        def _():
            own_to(1, q, 1, 0).start()

        @pl.when((z == 2) & second)
        def _():
            own_to(2, q, 0, 0).start()
            own_to(2, q, 1, 3).start()

        @pl.when(z == 3)
        def _():
            own_to(3, q, 0, 2 - 2 * m).start()

    def relay(i):
        s = i + groups * m
        arrived(0, s)
        pass_on(s, 0, 2).start()

    def relay_if(condition, i):
        @pl.when((z == 1) & condition)
        def _():
            relay(i)

    def send_range(block, begin, end, lane, device):
        @pl.loop(begin, end)
        def _(s):
            own_to(block, s, lane, device).start()

    constants[0].wait()
    whiten_inner(0)
    pl.semaphore_wait(barrier, 2 * blocks)

    @pl.when(sends_edge)
    def _():
        edge().start()

    send_inner(0)

    @pl.when(z == 0)
    def _():
        for device in range(1, blocks):
            flags_to(0, device, device - 1).start()

    @pl.when(z == 2)
    def _():
        flags_to(1, 3, 0).start()

    @pl.when(~takes_edge)
    def _():
        x_ref[:, :, :, edge_lanes] = jnp.zeros((2, windows, channels, EDGE), x_ref.dtype)

    def inner_step(q, carry):
        whiten_inner(q)
        send_inner(q)
        relay_if((q >= 3) & (lax.rem(q, 2) == 1), lax.div(q - 3, 2))
        return carry

    lax.fori_loop(1, groups, inner_step, 0)

    @pl.when(z == 0)
    def _():
        send_range(0, groups + groups * m, 3 * groups, 0, 1)

    @pl.when((z == 2) & second)
    def _():
        send_range(2, groups, 2 * groups, 1, 3)

    @pl.when((z == 3) & second)
    def _():
        send_range(3, 2 * groups, 3 * groups, 0, 2)

    @pl.when(takes_edge)
    def _():
        edge().wait_recv()

    def last_step(q, carry):
        whiten(q, (1 - mirrored) * (bands - 1) * BAND, 1, lambda j: bands - 1)
        s = (bands - 1) * groups + q

        @pl.when(z == 0)
        def _():
            own_to(0, s, 0, 1).start()

        @pl.when((z == 2) & first)
        def _():
            own_to(2, s, 0, 1).start()
            own_to(2, s, 1, 3).start()

        @pl.when(z == 3)
        def _():
            own_to(3, s, 0, 1 + m).start()

        relay_if(lax.rem(q, 4) == 3, 3 + lax.div(q, 4))
        return carry

    lax.fori_loop(0, groups, last_step, 0)

    @pl.when((z == 3) & first)
    def _():
        send_range(3, groups, 3 * groups, 0, 2)

    constants[1].wait()
    constants[2].wait()

    def transform(buffer, s):
        wide = jnp.concatenate([buffer[s, i] for i in range(GROUP)], axis=1)
        return jnp.dot(forward_ref[...], jnp.concatenate([wide, wide], axis=0), preferred_element_type=F32)

    tile = 32

    def power_into(total, s):
        for k in range(0, points, tile):
            gained = total[k : k + tile]
            for i in range(GROUP):
                lanes = slice(i * BAND, (i + 1) * BAND)
                real = spec[s, k : k + tile, lanes]
                imag = spec[s, points + k : points + k + tile, lanes]
                gained = gained + (real * real + imag * imag)
            total[k : k + tile] = gained

    def cross_into(total, near, far):
        for k in range(0, points, tile):
            gained_real = total[k : k + tile]
            gained_imag = total[points + k : points + k + tile]
            for i in range(GROUP):
                lanes = slice(i * BAND, (i + 1) * BAND)
                near_real = near[k : k + tile, lanes]
                near_imag = near[points + k : points + k + tile, lanes]
                far_real = far[k : k + tile, lanes]
                far_imag = far[points + k : points + k + tile, lanes]
                gained_real = gained_real + (near_real * far_real + near_imag * far_imag)
                gained_imag = gained_imag + (near_imag * far_real - near_real * far_imag)
            total[k : k + tile] = gained_real
            total[points + k : points + k + tile] = gained_imag

    def lags_of(values, columns):
        high = values.astype(BF16)
        low = (values - high.astype(F32)).astype(BF16)
        table = inverse_ref[:, :columns]
        rest = inverse_ref[:, 2 * points : 2 * points + columns]
        return jnp.dot(
            jnp.concatenate([table, rest, table], axis=1),
            jnp.concatenate([high, high, low], axis=0),
            preferred_element_type=F32,
        )

    def lags_of_many(*totals):
        both = lags_of(jnp.concatenate([total[...] for total in totals], axis=1), 2 * points)
        return [both[:, i * BAND : (i + 1) * BAND] for i in range(len(totals))]

    def add_piece(c, begin, piece):
        rows = pl.ds(begin, points)
        stack[c, 0, rows] += piece[:points]
        stack[c, 1, rows] += piece[points:]

    def clear(*totals):
        for total in totals:
            total[...] = jnp.zeros_like(total)

    def over_windows(step):
        def body(q, carry):
            step(q)
            return carry

        lax.fori_loop(0, groups, body, 0)

    def over_bands(begin, end, band):
        def body(c, carry):
            band(c)
            return carry

        lax.fori_loop(begin, end, body, 0)

    def own_band(c):
        clear(sums_a)

        def step(q):
            s = c * groups + q
            spec[s] = transform(white, s)
            power_into(sums_a, s)

        over_windows(step)
        stack[c] = jnp.zeros(stack.shape[1:], F32)
        add_piece(c, 0, flag_ref[REACH + 1 : REACH + 2, :] * lags_of(sums_a[:points], points))
        relay_if(c >= 0, EARLY - bands + c)

    over_bands(0, bands, own_band)

    def owner_of(flags, offset):
        return flags[offset : offset + 1, :]

    def far_share(flags, offset):
        return owner_of(flags, offset) * flags[REACH + 1 + offset : REACH + 2 + offset, :]

    def near_share(flags, offset):
        return (1.0 - owner_of(flags, offset)) * flags[REACH + 1 + offset : REACH + 2 + offset, :]

    def store_rows(buffer, c, begin, piece, rows=slice(0, 2 * channels)):
        count = rows.stop - rows.start
        for part in range(2):
            top = part * points
            buffer[c, part, begin : begin + count] = piece[top + rows.start : top + rows.stop].astype(buffer.dtype)

    def store_sums(buffer, c, parts):
        for part in range(2):
            top = part * points
            for k in range(len(parts) + 1):
                terms = []
                if k < len(parts):
                    terms.append(parts[k][top : top + channels])
                if k > 0:
                    terms.append(parts[k - 1][top + channels : top + points])
                total = terms[0] if len(terms) == 1 else terms[0] + terms[1]
                buffer[c, part, k * channels : (k + 1) * channels] = total.astype(buffer.dtype)

    zero_flags, two_flags = seen.at[0], seen.at[1]

    @pl.when(z == 0)
    def _():
        @pl.when(second)
        def _():
            clear(sums_a, sums_b, sums_c)

            def step(q):
                for block, total, held in ((1, sums_a, one), (2, sums_b, two), (3, sums_c, three)):
                    arrived(block, q)
                    held[...] = transform(received[block], q)
                    cross_into(total, spec.at[q], held)

            over_windows(step)
            pairs = lags_of_many(sums_a, sums_b, sums_c)
            for offset in range(1, REACH + 1):
                add_piece(0, offset * channels, near_share(flag_ref, offset) * pairs[offset - 1])
            store_rows(near_out, 0, 0, far_share(flag_ref, 1) * pairs[0])
            store_rows(far_out, 0, 0, far_share(flag_ref, 2) * pairs[1])
            store_rows(far_out, 0, points, far_share(flag_ref, 3) * pairs[2])
            start_all(far_pair_01(0, 0))
            start_all(far_pair_02(0, 0))
            start_all(far_pair_03(0, 0))

        @pl.loop(0, bands)
        def _(c):
            swap(c).start()

    @pl.when(z == 1)
    def _():
        flags_to(0, 1, 0).wait_recv()

        @pl.when(second)
        def _():
            swap(0).start()

        def band(c):
            clear(sums_a)

            def step(q):
                s = c * groups + q
                i = s - groups * m

                @pl.when(i + EARLY < 3 * groups)
                def _():
                    relay(i + EARLY)

                one[...] = transform(white0, s)
                cross_into(sums_a, one, spec.at[s])

                @pl.when(first & (c == bands - 2))
                def _():
                    late = (bands - 1) * groups + q
                    arrived(2, late)
                    spec[q] = transform(white2, late)
                    arrived(3, late)
                    spec[groups + q] = transform(white3, late)

            over_windows(step)
            piece = lags_of(sums_a[...], 2 * points)
            store_rows(near_out, c, 0, near_share(zero_flags, 1) * piece)
            start_all(near_from_1(c))
            add_piece(c, channels, far_share(zero_flags, 1) * piece)
            swap(c).start()

        over_bands(m, m + bands - 1, band)

        @pl.when(first)
        def _():
            c = bands - 1
            clear(sums_a, sums_b, sums_c)

            def step(q):
                s = c * groups + q
                arrived(0, s)
                one[...] = transform(white0, s)
                cross_into(sums_a, one, spec.at[s])
                cross_into(sums_b, one, spec.at[q])
                cross_into(sums_c, one, spec.at[groups + q])

            over_windows(step)
            pairs = lags_of_many(sums_a, sums_b, sums_c)
            store_sums(near_out, c, [near_share(zero_flags, o) * pairs[o - 1] for o in range(1, REACH + 1)])
            start_all(near_from_1_all(c))
            store_rows(far_out, c, points, far_share(zero_flags, 3) * pairs[2])
            start_all(far_pair_03(c, 1))
            store_rows(far_out, c, 0, far_share(zero_flags, 2) * pairs[1])
            start_all(far_pair_02(c, 1))
            add_piece(c, channels, far_share(zero_flags, 1) * pairs[0])
            swap(c).start()

    @pl.when(z == 2)
    def _():
        flags_to(0, 2, 0).wait_recv()

        @pl.when(first)
        def _():
            swap(bands - 1).start()

        @pl.when(second)
        def _():
            swap(0).start()
            clear(sums_a)

            def step(q):
                s = groups + q
                arrived(0, s)
                pass_on(s, 2, 3).start()
                one[...] = transform(white0, s)
                cross_into(sums_a, one, spec.at[s])

            over_windows(step)
            piece = lags_of(sums_a[...], 2 * points)
            store_rows(near_out, 1, 0, near_share(zero_flags, 2) * piece)
            near_out[1, :, points : points + channels] = jnp.zeros((2, channels, BAND), near_out.dtype)
            start_all(near_from_2(1))
            add_piece(1, 2 * channels, far_share(zero_flags, 2) * piece)
            swap(1).start()

        def band(c):
            clear(sums_a, sums_b, sums_c)

            def step(q):
                s = c * groups + q
                arrived(3, s)
                three[...] = transform(white3, s)
                cross_into(sums_b, spec.at[s], three)

                @pl.when(q == groups - 1)
                def _():
                    sums_b[...] = lags_of(sums_b[...], 2 * points)

                arrived(0, s)
                one[...] = transform(white0, s)
                cross_into(sums_a, one, spec.at[s])
                cross_into(sums_c, one, three)

            over_windows(step)
            near, beyond = lags_of_many(sums_a, sums_c)
            store_sums(near_out, c, [near_share(zero_flags, 2) * near, near_share(zero_flags, 3) * beyond])
            start_all(near_from_2(c))
            ahead = sums_b[...]
            store_rows(far_out, c, 0, far_share(flag_ref, 1) * ahead)
            store_rows(far_out, c, points, far_share(zero_flags, 3) * beyond)
            start_all(far_from_2(c))
            add_piece(c, 2 * channels, far_share(zero_flags, 2) * near)
            add_piece(c, channels, near_share(flag_ref, 1) * ahead)
            swap(c).start()

        over_bands(2 * m, bands - 1 + m, band)

    @pl.when(z == 3)
    def _():
        flags_to(0, 3, 0).wait_recv()
        flags_to(1, 3, 0).wait_recv()

        @pl.when(first)
        def _():
            @pl.loop(0, bands - 1)
            def _(c):
                swap(c).start()

        @pl.when(second)
        def _():
            @pl.loop(2, bands)
            def _(c):
                swap(c).start()

        def band(c):
            clear(sums_a)

            def step(q):
                s = c * groups + q
                arrived(2, s)
                two[...] = transform(white2, s)
                cross_into(sums_a, two, spec.at[s])

            over_windows(step)
            piece = lags_of(sums_a[...], 2 * points)
            store_rows(far_out, c, 0, near_share(two_flags, 1) * piece)
            start_all(near_pair_23(c))
            add_piece(c, channels, far_share(two_flags, 1) * piece)

            @pl.when(second & (c == 1))
            def _():
                clear(sums_c)

                def late_step(q):
                    s = c * groups + q
                    arrived(0, s)
                    one[...] = transform(white0, s)
                    cross_into(sums_c, one, spec.at[s])

                over_windows(late_step)
                distant = lags_of(sums_c[...], 2 * points)
                store_rows(near_out, c, points, near_share(zero_flags, 3) * distant)
                start_all(near_from_3(c))
                add_piece(c, 3 * channels, far_share(zero_flags, 3) * distant)

            swap(c).start()

        over_bands((1 - m) * (bands - 1), (1 - m) * bands + 2 * m, band)

    def lanes_of(core, c):
        return pl.ds(pl.multiple_of(core * half + place(c) * BAND, BAND), BAND)

    def collect(c):
        out_ref[:, :, lanes_of(m, c)] = stack[c, :, pl.ds(pl.multiple_of(m * kept, 8), kept)]
        swap(c).wait_recv()
        out_ref[:, :, lanes_of(1 - m, c)] = swapped[c]
        swap(c).wait_send()

    over_bands(0, bands, collect)

    def take(target, c, source, sender, low, high):
        top, end = max(low, target * kept), min(high, (target + 1) * kept)
        if top < end:
            rows = slice(top - target * kept, end - target * kept)
            results(c, source, sender, near_out, low, low, high, 0, 0)[target].wait_recv()
            out_ref[:, rows, lanes_of(sender, c)] += inbox[source, sender, c, :, rows].astype(F32)

    def take_at_0(target):
        for sender in range(halves):
            def band(c):
                take(target, c, 1, sender, channels, one_pair)
                take(target, c, 2, sender, 2 * channels, three_pairs)

            over_bands(sender, sender + bands - 1, band)
        take(target, 1, 3, 1, 3 * channels, three_pairs)
        take(target, bands - 1, 1, 0, channels, three_pairs)

    def take_at_1(target):
        take(target, 0, 0, 1, channels, one_pair)

    def take_at_2(target):
        take(target, 0, 0, 1, 2 * channels, two_pairs)
        take(target, 0, 3, 1, channels, one_pair)
        take(target, 1, 3, 1, channels, one_pair)
        take(target, bands - 1, 3, 0, channels, one_pair)
        take(target, bands - 1, 1, 0, 2 * channels, two_pairs)

    def take_at_3(target):
        take(target, 0, 0, 1, 3 * channels, three_pairs)
        for sender in range(halves):
            def band(c):
                take(target, c, 2, sender, channels, three_pairs)

            over_bands(2 * sender, bands - 1 + sender, band)
        take(target, bands - 1, 1, 0, 3 * channels, three_pairs)

    for block, step in enumerate((take_at_0, take_at_1, take_at_2, take_at_3)):
        for target in range(halves):
            @pl.when((z == block) & (m == target))
            def _():
                step(target)

    @pl.when(sends_edge)
    def _():
        edge().wait_send()

    def sent_range(begin, end, lane):
        @pl.loop(begin, end)
        def _(s):
            sent(s, lane)

    @pl.when(z == 0)
    def _():
        for device in range(1, blocks):
            flags_to(0, device, device - 1).wait_send()
        sent_range(groups * m, pieces, 0)

        @pl.when(second)
        def _():
            finish_all(far_pair_01(0, 0))
            finish_all(far_pair_02(0, 0))
            finish_all(far_pair_03(0, 0))

    @pl.when(z == 1)
    def _():
        sent_range(groups * m, groups * m + 3 * groups, 0)
        over_bands(m, m + bands - 1, lambda c: finish_all(near_from_1(c)))

        @pl.when(second)
        def _():
            sent_range(0, groups, 1)

        @pl.when(first)
        def _():
            finish_all(near_from_1_all(bands - 1))
            finish_all(far_pair_03(bands - 1, 1))
            finish_all(far_pair_02(bands - 1, 1))

    @pl.when(z == 2)
    def _():
        flags_to(1, 3, 0).wait_send()

        @pl.when(first)
        def _():
            sent_range((bands - 1) * groups, pieces, 0)
            sent_range((bands - 1) * groups, pieces, 1)

        @pl.when(second)
        def _():
            sent_range(0, groups, 0)
            sent_range(0, 2 * groups, 1)
            sent_range(groups, 2 * groups, 2)
            finish_all(near_from_2(1))

        def band(c):
            finish_all(near_from_2(c))
            finish_all(far_from_2(c))

        over_bands(2 * m, bands - 1 + m, band)

    @pl.when(z == 3)
    def _():
        @pl.when(first)
        def _():
            sent_range(0, pieces, 0)
            finish_all(near_pair_23(bands - 1))

        @pl.when(second)
        def _():
            sent_range(0, groups, 0)
            sent_range(2 * groups, pieces, 0)
            finish_all(near_pair_23(0))
            finish_all(near_pair_23(1))
            finish_all(near_from_3(1))


def four_block_shards(spectra, counts, owners):
    parts, windows, channels, bins = spectra.shape
    halves, blocks = lax.axis_size("pairs"), lax.axis_size("cable")
    half, points = bins // halves, 2 * channels
    forward, inverse = channel_transforms(channels, 1.0 / math.sqrt(windows * channels))
    window = smoothing_window()
    bands, groups = half // BAND, windows // GROUP
    pieces = bands * groups
    rows = (REACH + 2) * channels
    kept = rows // halves
    block = pltpu.VMEM((pieces, GROUP, points, BAND), BF16)
    spectrum = pltpu.VMEM((2 * points, GROUP * BAND), F32)
    sums = pltpu.VMEM((2 * points, BAND), F32)
    shares = pltpu.VMEM((bands, 2, 2 * points, BAND), BF16)
    flags = (2 * (REACH + 1), BAND)
    dma = pltpu.SemaphoreType.DMA
    width = inverse.shape[1]
    tables = np.zeros((TABLE_ROWS, width), jnp.bfloat16)
    top = 0
    for table in (window, forward, inverse):
        tables[top : top + table.shape[0], : table.shape[1]] = table
        top += table.shape[0]
    hbm = pl.BlockSpec(memory_space=pl.ANY)
    smem = pl.BlockSpec(memory_space=pltpu.SMEM)
    out = pl.pallas_call(
        stack_kernel,
        out_shape=jax.ShapeDtypeStruct((2, kept, bins), F32),
        in_specs=[hbm, smem, smem, hbm],
        out_specs=pl.BlockSpec(memory_space=pltpu.VMEM),
        scratch_shapes=[
            pltpu.VMEM((2, windows, channels, half + 2 * EDGE), BF16),
            pltpu.VMEM(window.shape, BF16),
            pltpu.VMEM(forward.shape, BF16),
            pltpu.VMEM(inverse.shape, BF16),
            pltpu.VMEM(flags, F32),
            pltpu.VMEM((2,) + flags, F32),
            block, block, block, block, block,
            pltpu.VMEM((pieces, 2 * points, GROUP * BAND), F32),
            spectrum, spectrum, spectrum, sums, sums, sums,
            pltpu.VMEM((bands, 2, rows, BAND), F32),
            shares, shares,
            pltpu.VMEM((blocks, halves, bands, 2, kept, BAND), BF16),
            pltpu.VMEM((bands, 2, kept, BAND), F32),
            dma((groups,)), dma((3,)), dma((1,)), dma((1,)), dma((3,)), dma((2,)),
            dma((3, pieces)), dma((blocks, pieces)),
            dma((3, halves, bands)), dma((blocks, halves, bands)),
            dma((bands,)), dma((bands,)),
        ],
        compiler_params=pltpu.CompilerParams(
            collective_id=0, has_side_effects=True, vmem_limit_bytes=55000000
        ),
    )(spectra, counts, owners, jnp.asarray(tables))
    return out[:, None]


def solution(mesh):
    sizes = dict(mesh.shape)
    fits = sizes["cable"] == REACH + 1 and sizes["pairs"] == 2 and sizes["bins"] == 2
    shards = four_block_shards if fits else general_shards
    placed = (
        P("groups", None, "cable", "bins"),
        P(("groups", "cable")),
        P(("groups", "cable"), None),
    )
    return jax.shard_map(
        shards,
        mesh=mesh,
        in_specs=placed,
        out_specs=P("groups", "cable", "pairs", "bins"),
        check_vma=False,
    )
```

time: 70.7 us -> 60 us (0.85)
  Pallas kernels: 67.4 us -> 57.4 us
  local copies, waits for them, and re-layouts: 2.52 us -> 1.71 us
    pallas_call x1, Pallas kernels: 67.4 us -> 57.4 us  [four_block_shards(): pl.pallas_call(stack_kernel, out_shape=jax.ShapeDtypeStruct((2, kept, bin...]
    unnamed x1 -> x3, local copies, waits for them, and re-layouts: 2.52 us -> 1.71 us
where the time goes in v1:
time: 60 us; the launch traced here: 59.8 us
  Pallas kernels  57.4 us (96%)
  local copies, waits for them, and re-layouts  1.71 us (3%)
  between operations  0.67 us (1%)
    pallas_call x1, Pallas kernels, four_block_shards(): pl.pallas_call(stack_kernel, out_shape=jax.ShapeDtypeStruct((2, kept, bin...  57.4 us
    unnamed x3, local copies, waits for them, and re-layouts  1.71 us

profile of v1, /device:TPU:1, one launch (start us, length us, event | category | flops | bytes accessed | tf_op | source)
XLA Modules:
  0.0 59.8 jit_solution(9423910479589361523)
XLA Ops:
  0.7 0.0 copy-start
  0.7 0.6 %copy-done = s32[1,4]{1,0:T(1,128)S(1)} copy-done((s32[1,4]{1,0:T(1,128)S(1)}, s32[1,4]{1,0:T(1,128)}, u32[]{:S(2)}) %copy-start) | copy-done | bytes 40
  1.3 57.4 %shard_map.46 = f32[2,160,1024]{2,1,0:T(8,128)S(1)} custom-call(bf16[2,16,64,1024]{3,2,1,0:T(8,128)(2,1)} %spectra_ref.1, s32[1]{0:T(128)S(6)} %copy.7.counts_ref, s32[1,4]{1,0:T(1,128)S(1)} %copy-done, bf16[2048,512]{1,0:T(8,128)(2,1)} %constant.2.clone.tables_ref), custom_call_target="tpu_custom_call" | custom-call | tf_op jit(solution)/shard_map/pallas_call | solution.py:927
  58.7 1.1 %copy.8 = f32[2,1,160,1024]{3,2,1,0:T(8,128)} copy(f32[2,1,160,1024]{3,2,1,0:T(8,128)S(1)} %bitcast.3) | data formatting | bytes 2621440
Async XLA Ops:
  0.7 0.7 %copy-start = (s32[1,4]{1,0:T(1,128)S(1)}, s32[1,4]{1,0:T(1,128)}, u32[]{:S(2)}) copy-start(s32[1,4]{1,0:T(1,128)} %owners_ref.1) | copy-start | bytes 52

commit v2 on v1

--- a/solution.py
+++ b/solution.py
@@ -164,7 +164,7 @@
     white, white0, white1, white2, white3, spec, one, two, three, sums_a, sums_b, sums_c,
     stack, near_out, far_out, inbox, swapped,
     load_sem, constant_sem, edge_send, edge_recv, flag_send, flag_recv,
-    block_send, block_recv, result_send, result_recv, swap_send, swap_recv,
+    block_send, block_recv, result_send, result_recv, swap_send, swap_recv, known, spread, drained,
 ):
     windows, channels = x_ref.shape[1:3]
     half = x_ref.shape[3] - 2 * EDGE
@@ -306,14 +306,22 @@
     constants[2].start()
     live = jnp.minimum(counts_ref[0], blocks - z)
     for offset in range(REACH + 1):
-        flag_ref[offset : offset + 1, :] = jnp.full((1, BAND), owners_ref[0, offset].astype(F32))
+        flag_ref[offset : offset + 1, :] = jnp.full((1, BAND), owners_ref[offset].astype(F32))
         weight = jnp.where(offset < live, 1.0, 0.0)
         flag_ref[REACH + 1 + offset : REACH + 2 + offset, :] = jnp.full((1, BAND), weight)
     barrier = pltpu.get_barrier_semaphore()
-    for step in range(1, blocks):
-        pl.semaphore_signal(barrier, inc=1, device_id={"cable": lax.rem(z + step, blocks)}, device_id_type=MESH)
-        across = {"cable": lax.rem(z + step, blocks), "pairs": 1 - m}
-        pl.semaphore_signal(barrier, inc=1, device_id=across, device_id_type=MESH)
+    beside = jnp.where((z > 0) & (z < blocks - 1), 2, 1)
+
+    def tell_beside(semaphore):
+        @pl.when(z > 0)
+        def _():
+            pl.semaphore_signal(semaphore, inc=1, device_id={"cable": z - 1}, device_id_type=MESH)
+
+        @pl.when(z < blocks - 1)
+        def _():
+            pl.semaphore_signal(semaphore, inc=1, device_id={"cable": z + 1}, device_id_type=MESH)
+
+    tell_beside(barrier)
     pl.semaphore_signal(barrier, inc=1, device_id=partner, device_id_type=MESH)
     pl.semaphore_signal(barrier, inc=1, device_id={"bins": 1 - x}, device_id_type=MESH)
     sends_edge = x == m
@@ -358,14 +366,13 @@
         def _():
             own_to(1, q, 1, 0).start()
 
-        @pl.when((z == 2) & second)
-        def _():
-            own_to(2, q, 0, 0).start()
+        @pl.when(z == 2)
+        def _():
             own_to(2, q, 1, 3).start()
 
         @pl.when(z == 3)
         def _():
-            own_to(3, q, 0, 2 - 2 * m).start()
+            own_to(3, q + groups * (1 + m), 0, 2).start()
 
     def relay(i):
         s = i + groups * m
@@ -384,7 +391,8 @@
 
     constants[0].wait()
     whiten_inner(0)
-    pl.semaphore_wait(barrier, 2 * blocks)
+    pl.semaphore_wait(barrier, beside + 2)
+    tell_beside(known)
 
     @pl.when(sends_edge)
     def _():
@@ -394,8 +402,7 @@
 
     @pl.when(z == 0)
     def _():
-        for device in range(1, blocks):
-            flags_to(0, device, device - 1).start()
+        flags_to(0, 1, 0).start()
 
     @pl.when(z == 2)
     def _():
@@ -411,19 +418,26 @@
         relay_if((q >= 3) & (lax.rem(q, 2) == 1), lax.div(q - 3, 2))
         return carry
 
-    lax.fori_loop(1, groups, inner_step, 0)
+    lax.fori_loop(1, groups // 2, inner_step, 0)
+    pl.semaphore_wait(known, beside)
+    tell_beside(spread)
+    lax.fori_loop(groups // 2, groups, inner_step, 0)
+    pl.semaphore_wait(spread, beside)
 
     @pl.when(z == 0)
     def _():
+        for device in range(2, blocks):
+            flags_to(0, device, device - 1).start()
         send_range(0, groups + groups * m, 3 * groups, 0, 1)
 
     @pl.when((z == 2) & second)
     def _():
+        send_range(2, 0, groups, 0, 0)
         send_range(2, groups, 2 * groups, 1, 3)
 
     @pl.when((z == 3) & second)
     def _():
-        send_range(3, 2 * groups, 3 * groups, 0, 2)
+        send_range(3, 0, groups, 0, 0)
 
     @pl.when(takes_edge)
     def _():
@@ -453,7 +467,7 @@
 
     @pl.when((z == 3) & first)
     def _():
-        send_range(3, groups, 3 * groups, 0, 2)
+        send_range(3, 2 * groups, 3 * groups, 0, 2)
 
     constants[1].wait()
     constants[2].wait()
@@ -590,13 +604,22 @@
             store_rows(near_out, 0, 0, far_share(flag_ref, 1) * pairs[0])
             store_rows(far_out, 0, 0, far_share(flag_ref, 2) * pairs[1])
             store_rows(far_out, 0, points, far_share(flag_ref, 3) * pairs[2])
-            start_all(far_pair_01(0, 0))
-            start_all(far_pair_02(0, 0))
-            start_all(far_pair_03(0, 0))
 
         @pl.loop(0, bands)
         def _(c):
             swap(c).start()
+
+        @pl.when(first)
+        def _():
+            sent(pieces - 1, 0)
+            pl.semaphore_signal(drained, inc=1, device_id=partner, device_id_type=MESH)
+
+        @pl.when(second)
+        def _():
+            pl.semaphore_wait(drained, 1)
+            start_all(far_pair_03(0, 0))
+            start_all(far_pair_02(0, 0))
+            start_all(far_pair_01(0, 0))
 
     @pl.when(z == 1)
     def _():
@@ -672,22 +695,23 @@
         @pl.when(second)
         def _():
             swap(0).start()
-            clear(sums_a)
-
-            def step(q):
-                s = groups + q
-                arrived(0, s)
-                pass_on(s, 2, 3).start()
-                one[...] = transform(white0, s)
-                cross_into(sums_a, one, spec.at[s])
-
-            over_windows(step)
-            piece = lags_of(sums_a[...], 2 * points)
-            store_rows(near_out, 1, 0, near_share(zero_flags, 2) * piece)
-            near_out[1, :, points : points + channels] = jnp.zeros((2, channels, BAND), near_out.dtype)
-            start_all(near_from_2(1))
-            add_piece(1, 2 * channels, far_share(zero_flags, 2) * piece)
-            swap(1).start()
+
+        clear(sums_a)
+
+        def early_step(q):
+            s = m * groups + q
+            arrived(0, s)
+            pass_on(s, 2, 3).start()
+            one[...] = transform(white0, s)
+            cross_into(sums_a, one, spec.at[s])
+
+        over_windows(early_step)
+        piece = lags_of(sums_a[...], 2 * points)
+        store_rows(near_out, m, 0, near_share(zero_flags, 2) * piece)
+        near_out[m, :, points : points + channels] = jnp.zeros((2, channels, BAND), near_out.dtype)
+        start_all(near_from_2(m))
+        add_piece(m, 2 * channels, far_share(zero_flags, 2) * piece)
+        swap(m).start()
 
         def band(c):
             clear(sums_a, sums_b, sums_c)
@@ -719,24 +743,16 @@
             add_piece(c, channels, near_share(flag_ref, 1) * ahead)
             swap(c).start()
 
-        over_bands(2 * m, bands - 1 + m, band)
+        over_bands(1 + m, bands - 1 + m, band)
 
     @pl.when(z == 3)
     def _():
         flags_to(0, 3, 0).wait_recv()
         flags_to(1, 3, 0).wait_recv()
 
-        @pl.when(first)
-        def _():
-            @pl.loop(0, bands - 1)
-            def _(c):
-                swap(c).start()
-
-        @pl.when(second)
-        def _():
-            @pl.loop(2, bands)
-            def _(c):
-                swap(c).start()
+        @pl.loop(1 + m, bands - 1 + m)
+        def _(c):
+            swap(c).start()
 
         def band(c):
             clear(sums_a)
@@ -753,7 +769,7 @@
             start_all(near_pair_23(c))
             add_piece(c, channels, far_share(two_flags, 1) * piece)
 
-            @pl.when(second & (c == 1))
+            @pl.when(c == m)
             def _():
                 clear(sums_c)
 
@@ -771,7 +787,7 @@
 
             swap(c).start()
 
-        over_bands((1 - m) * (bands - 1), (1 - m) * bands + 2 * m, band)
+        over_bands(0, 2, lambda i: band(i * (bands - 1 - (bands - 2) * m)))
 
     def lanes_of(core, c):
         return pl.ds(pl.multiple_of(core * half + place(c) * BAND, BAND), BAND)
@@ -798,7 +814,7 @@
                 take(target, c, 2, sender, 2 * channels, three_pairs)
 
             over_bands(sender, sender + bands - 1, band)
-        take(target, 1, 3, 1, 3 * channels, three_pairs)
+            take(target, sender, 3, sender, 3 * channels, three_pairs)
         take(target, bands - 1, 1, 0, channels, three_pairs)
 
     def take_at_1(target):
@@ -808,6 +824,7 @@
         take(target, 0, 0, 1, 2 * channels, two_pairs)
         take(target, 0, 3, 1, channels, one_pair)
         take(target, 1, 3, 1, channels, one_pair)
+        take(target, 0, 3, 0, channels, one_pair)
         take(target, bands - 1, 3, 0, channels, one_pair)
         take(target, bands - 1, 1, 0, 2 * channels, two_pairs)
 
@@ -817,7 +834,7 @@
             def band(c):
                 take(target, c, 2, sender, channels, three_pairs)
 
-            over_bands(2 * sender, bands - 1 + sender, band)
+            over_bands(1 + sender, bands - 1 + sender, band)
         take(target, bands - 1, 1, 0, 3 * channels, three_pairs)
 
     for block, step in enumerate((take_at_0, take_at_1, take_at_2, take_at_3)):
@@ -839,7 +856,7 @@
     def _():
         for device in range(1, blocks):
             flags_to(0, device, device - 1).wait_send()
-        sent_range(groups * m, pieces, 0)
+        sent_range(groups * m, pieces - 1 + m, 0)
 
         @pl.when(second)
         def _():
@@ -874,21 +891,22 @@
         @pl.when(second)
         def _():
             sent_range(0, groups, 0)
-            sent_range(0, 2 * groups, 1)
-            sent_range(groups, 2 * groups, 2)
-            finish_all(near_from_2(1))
+
+        sent_range(0, groups + groups * m, 1)
+        sent_range(groups * m, groups + groups * m, 2)
+        finish_all(near_from_2(m))
 
         def band(c):
             finish_all(near_from_2(c))
             finish_all(far_from_2(c))
 
-        over_bands(2 * m, bands - 1 + m, band)
+        over_bands(1 + m, bands - 1 + m, band)
 
     @pl.when(z == 3)
     def _():
         @pl.when(first)
         def _():
-            sent_range(0, pieces, 0)
+            sent_range(groups, pieces, 0)
             finish_all(near_pair_23(bands - 1))
 
         @pl.when(second)
@@ -896,8 +914,9 @@
             sent_range(0, groups, 0)
             sent_range(2 * groups, pieces, 0)
             finish_all(near_pair_23(0))
-            finish_all(near_pair_23(1))
-            finish_all(near_from_3(1))
+
+        finish_all(near_pair_23(m))
+        finish_all(near_from_3(m))
 
 
 def four_block_shards(spectra, counts, owners):
@@ -947,11 +966,12 @@
             dma((3, pieces)), dma((blocks, pieces)),
             dma((3, halves, bands)), dma((blocks, halves, bands)),
             dma((bands,)), dma((bands,)),
+            pltpu.SemaphoreType.REGULAR, pltpu.SemaphoreType.REGULAR, pltpu.SemaphoreType.REGULAR,
         ],
         compiler_params=pltpu.CompilerParams(
             collective_id=0, has_side_effects=True, vmem_limit_bytes=55000000
         ),
-    )(spectra, counts, owners, jnp.asarray(tables))
+    )(spectra, counts, owners.reshape(-1), jnp.asarray(tables))
     return out[:, None]
 
 

time: 60 us -> 56.9 us (0.948)
  Pallas kernels: 57.4 us -> 54.4 us
    pallas_call x1, Pallas kernels: 57.4 us -> 54.4 us  [four_block_shards(): pl.pallas_call(stack_kernel, out_shape=jax.ShapeDtypeStruct((2, kept, bin...]
where the time goes in v2:
time: 56.9 us; the launch traced here: 56.8 us
  Pallas kernels  54.4 us (96%)
  local copies, waits for them, and re-layouts  1.71 us (3%)
  between operations  0.67 us (1%)
    pallas_call x1, Pallas kernels, four_block_shards(): pl.pallas_call(stack_kernel, out_shape=jax.ShapeDtypeStruct((2, kept, bin...  54.4 us
    unnamed x3, local copies, waits for them, and re-layouts  1.71 us

profile of v2, /device:TPU:1, one launch (start us, length us, event | category | flops | bytes accessed | tf_op | source)
XLA Modules:
  0.0 56.8 jit_solution(17239896608365507912)
XLA Ops:
  0.7 0.0 copy-start
  0.7 0.6 %copy-done = s32[1,4]{1,0:T(1,128)S(1)} copy-done((s32[1,4]{1,0:T(1,128)S(1)}, s32[1,4]{1,0:T(1,128)}, u32[]{:S(2)}) %copy-start) | copy-done | bytes 40
  1.3 54.4 %shard_map.46 = f32[2,160,1024]{2,1,0:T(8,128)S(1)} custom-call(bf16[2,16,64,1024]{3,2,1,0:T(8,128)(2,1)} %spectra_ref.1, s32[1]{0:T(128)S(6)} %copy.7.counts_ref, s32[4]{0:T(128)S(1)} %bitcast.5, bf16[2048,512]{1,0:T(8,128)(2,1)} %constant.2.clone.tables_ref), custom_call_target="tpu_custom_call" | custom-call | tf_op jit(solution)/shard_map/pallas_call | solution.py:946
  55.7 1.1 %copy.8 = f32[2,1,160,1024]{3,2,1,0:T(8,128)} copy(f32[2,1,160,1024]{3,2,1,0:T(8,128)S(1)} %bitcast.4) | data formatting | bytes 2621440
Async XLA Ops:
  0.7 0.7 %copy-start = (s32[1,4]{1,0:T(1,128)S(1)}, s32[1,4]{1,0:T(1,128)}, u32[]{:S(2)}) copy-start(s32[1,4]{1,0:T(1,128)} %param.6) | copy-start | bytes 52

commit v3 on v2

--- a/solution.py
+++ b/solution.py
@@ -127,6 +127,7 @@
 BAND = 128
 GROUP = 2
 EARLY = 9
+CATCH_UP = 14
 TABLE_ROWS = 2048
 F32 = jnp.float32
 BF16 = jnp.bfloat16
@@ -159,7 +160,8 @@
 
 
 def stack_kernel(
-    spectra_ref, counts_ref, owners_ref, tables_ref, out_ref,
+    spectra_ref, counts_ref, owners_hbm, tables_ref, out_ref,
+    owners_ref,
     x_ref, window_ref, forward_ref, inverse_ref, flag_ref, seen,
     white, white0, white1, white2, white3, spec, one, two, three, sums_a, sums_b, sums_c,
     stack, near_out, far_out, inbox, swapped,
@@ -281,16 +283,18 @@
         constants.append(pltpu.make_async_copy(source, table, constant_sem.at[i]))
         top += rows
 
-    edge_lanes = pl.ds(pl.multiple_of(m * (half + EDGE), EDGE), EDGE)
-
-    def edge():
-        source = pl.ds(pl.multiple_of((1 - m) * (bins - EDGE), EDGE), EDGE)
+    def edge_lanes(core):
+        return pl.ds(pl.multiple_of(core * (half + EDGE), EDGE), EDGE)
+
+    def edge(q):
+        begin = EDGE + (1 - x) * (half - EDGE)
+        rows = pl.ds(q * GROUP, GROUP)
         return remote(
-            spectra_ref.at[:, :, :, source],
-            x_ref.at[:, :, :, edge_lanes],
-            edge_send.at[0],
-            edge_recv.at[0],
-            {"bins": 1 - x},
+            x_ref.at[:, rows, :, pl.ds(pl.multiple_of(begin, EDGE), EDGE)],
+            x_ref.at[:, rows, :, edge_lanes(x)],
+            edge_send.at[q],
+            edge_recv.at[q],
+            {"bins": 1 - x, "pairs": x},
         )
 
     def flags_to(source, device, lane):
@@ -300,15 +304,12 @@
 
     load(0).start()
     constants[0].start()
+    settings = pltpu.make_async_copy(owners_hbm, owners_ref, flag_send.at[0])
+    settings.start()
     for q in range(1, groups):
         load(q).start()
     constants[1].start()
     constants[2].start()
-    live = jnp.minimum(counts_ref[0], blocks - z)
-    for offset in range(REACH + 1):
-        flag_ref[offset : offset + 1, :] = jnp.full((1, BAND), owners_ref[offset].astype(F32))
-        weight = jnp.where(offset < live, 1.0, 0.0)
-        flag_ref[REACH + 1 + offset : REACH + 2 + offset, :] = jnp.full((1, BAND), weight)
     barrier = pltpu.get_barrier_semaphore()
     beside = jnp.where((z > 0) & (z < blocks - 1), 2, 1)
 
@@ -323,9 +324,11 @@
 
     tell_beside(barrier)
     pl.semaphore_signal(barrier, inc=1, device_id=partner, device_id_type=MESH)
-    pl.semaphore_signal(barrier, inc=1, device_id={"bins": 1 - x}, device_id_type=MESH)
-    sends_edge = x == m
-    takes_edge = x != m
+    at_cut = x != m
+
+    @pl.when(at_cut)
+    def _():
+        pl.semaphore_signal(barrier, inc=1, device_id={"bins": 1 - x, "pairs": x}, device_id_type=MESH)
 
     def whiten(q, begin, count, store):
         lanes = pl.ds(pl.multiple_of(begin, BAND), count * BAND + 2 * EDGE)
@@ -354,17 +357,22 @@
                 white[slot, i, channels:] = (imags[i][:, here] * rows).astype(BF16)
 
     def whiten_inner(q):
-        load(q).wait()
         whiten(q, mirrored * BAND, bands - 1, lambda j: j + mirrored * (bands - 2 - 2 * j))
 
+    def send_edge(q):
+        @pl.when(at_cut)
+        def _():
+            edge(q).start()
+
+    def send_first(q):
+        @pl.when(z == 0)
+        def _():
+            own_to(0, q, 0, 1).start()
+
     def send_inner(q):
-        @pl.when(z == 0)
-        def _():
-            own_to(0, q + groups * m, 0, 1).start()
-
         @pl.when((z == 1) & second)
         def _():
-            own_to(1, q, 1, 0).start()
+            own_to(1, q + 2 * groups, 1, 0).start()
 
         @pl.when(z == 2)
         def _():
@@ -372,10 +380,10 @@
 
         @pl.when(z == 3)
         def _():
-            own_to(3, q + groups * (1 + m), 0, 2).start()
+            own_to(3, q + groups, 0, 2).start()
 
     def relay(i):
-        s = i + groups * m
+        s = i + groups * m * lax.div(i, 2 * groups)
         arrived(0, s)
         pass_on(s, 0, 2).start()
 
@@ -390,16 +398,22 @@
             own_to(block, s, lane, device).start()
 
     constants[0].wait()
-    whiten_inner(0)
-    pl.semaphore_wait(barrier, beside + 2)
+    load(0).wait()
+    whiten(0, mirrored * (bands - 1) * BAND, 1, lambda j: 0)
+    pl.semaphore_wait(barrier, beside + 1 + jnp.where(at_cut, 1, 0))
+    send_first(0)
+    send_edge(0)
     tell_beside(known)
-
-    @pl.when(sends_edge)
-    def _():
-        edge().start()
-
+    whiten(0, BAND, bands - 2, lambda j: 1 + j + mirrored * (bands - 3 - 2 * j))
     send_inner(0)
 
+    settings.wait()
+    live = jnp.minimum(counts_ref[0], blocks - z)
+    for offset in range(REACH + 1):
+        flag_ref[offset : offset + 1, :] = jnp.full((1, BAND), owners_ref[0, offset].astype(F32))
+        weight = jnp.where(offset < live, 1.0, 0.0)
+        flag_ref[REACH + 1 + offset : REACH + 2 + offset, :] = jnp.full((1, BAND), weight)
+
     @pl.when(z == 0)
     def _():
         flags_to(0, 1, 0).start()
@@ -408,12 +422,15 @@
     def _():
         flags_to(1, 3, 0).start()
 
-    @pl.when(~takes_edge)
-    def _():
-        x_ref[:, :, :, edge_lanes] = jnp.zeros((2, windows, channels, EDGE), x_ref.dtype)
+    @pl.when(~at_cut)
+    def _():
+        x_ref[:, :, :, edge_lanes(m)] = jnp.zeros((2, windows, channels, EDGE), x_ref.dtype)
 
     def inner_step(q, carry):
+        load(q).wait()
+        send_edge(q)
         whiten_inner(q)
+        send_first(q)
         send_inner(q)
         relay_if((q >= 3) & (lax.rem(q, 2) == 1), lax.div(q - 3, 2))
         return carry
@@ -428,46 +445,16 @@
     def _():
         for device in range(2, blocks):
             flags_to(0, device, device - 1).start()
-        send_range(0, groups + groups * m, 3 * groups, 0, 1)
+        send_range(0, groups, (3 - m) * groups, 0, 1)
 
     @pl.when((z == 2) & second)
     def _():
-        send_range(2, 0, groups, 0, 0)
-        send_range(2, groups, 2 * groups, 1, 3)
+        send_range(2, 2 * groups, 3 * groups, 0, 0)
+        send_range(2, 2 * groups, 3 * groups, 1, 3)
 
     @pl.when((z == 3) & second)
     def _():
-        send_range(3, 0, groups, 0, 0)
-
-    @pl.when(takes_edge)
-    def _():
-        edge().wait_recv()
-
-    def last_step(q, carry):
-        whiten(q, (1 - mirrored) * (bands - 1) * BAND, 1, lambda j: bands - 1)
-        s = (bands - 1) * groups + q
-
-        @pl.when(z == 0)
-        def _():
-            own_to(0, s, 0, 1).start()
-
-        @pl.when((z == 2) & first)
-        def _():
-            own_to(2, s, 0, 1).start()
-            own_to(2, s, 1, 3).start()
-
-        @pl.when(z == 3)
-        def _():
-            own_to(3, s, 0, 1 + m).start()
-
-        relay_if(lax.rem(q, 4) == 3, 3 + lax.div(q, 4))
-        return carry
-
-    lax.fori_loop(0, groups, last_step, 0)
-
-    @pl.when((z == 3) & first)
-    def _():
-        send_range(3, 2 * groups, 3 * groups, 0, 2)
+        send_range(3, 2 * groups, 3 * groups, 0, 0)
 
     constants[1].wait()
     constants[2].wait()
@@ -552,9 +539,41 @@
         over_windows(step)
         stack[c] = jnp.zeros(stack.shape[1:], F32)
         add_piece(c, 0, flag_ref[REACH + 1 : REACH + 2, :] * lags_of(sums_a[:points], points))
-        relay_if(c >= 0, EARLY - bands + c)
-
-    over_bands(0, bands, own_band)
+        relay_if(c >= 0, EARLY - bands - 2 + c + 2 * lax.div(c, bands - 1))
+
+    over_bands(0, bands - 1, own_band)
+
+    def last_step(q, carry):
+        @pl.when(at_cut)
+        def _():
+            edge(q).wait_recv()
+
+        whiten(q, (1 - mirrored) * (bands - 1) * BAND, 1, lambda j: bands - 1)
+        s = (bands - 1) * groups + q
+
+        @pl.when(z == 0)
+        def _():
+            own_to(0, s, 0, 1).start()
+
+        @pl.when((z == 2) & first)
+        def _():
+            own_to(2, s, 0, 1).start()
+            own_to(2, s, 1, 3).start()
+
+        @pl.when(z == 3)
+        def _():
+            own_to(3, s, 0, 1 + m).start()
+
+        relay_if(lax.rem(q, 4) == 3, EARLY - 3 + lax.div(q, 4))
+        return carry
+
+    lax.fori_loop(0, groups, last_step, 0)
+
+    @pl.when((z == 3) & first)
+    def _():
+        send_range(3, 2 * groups, 3 * groups, 0, 2)
+
+    over_bands(bands - 1, bands, own_band)
 
     def owner_of(flags, offset):
         return flags[offset : offset + 1, :]
@@ -593,17 +612,18 @@
 
             def step(q):
                 for block, total, held in ((1, sums_a, one), (2, sums_b, two), (3, sums_c, three)):
-                    arrived(block, q)
-                    held[...] = transform(received[block], q)
-                    cross_into(total, spec.at[q], held)
+                    s = 2 * groups + q
+                    arrived(block, s)
+                    held[...] = transform(received[block], s)
+                    cross_into(total, spec.at[s], held)
 
             over_windows(step)
             pairs = lags_of_many(sums_a, sums_b, sums_c)
             for offset in range(1, REACH + 1):
-                add_piece(0, offset * channels, near_share(flag_ref, offset) * pairs[offset - 1])
-            store_rows(near_out, 0, 0, far_share(flag_ref, 1) * pairs[0])
-            store_rows(far_out, 0, 0, far_share(flag_ref, 2) * pairs[1])
-            store_rows(far_out, 0, points, far_share(flag_ref, 3) * pairs[2])
+                add_piece(2, offset * channels, near_share(flag_ref, offset) * pairs[offset - 1])
+            store_rows(near_out, 2, 0, far_share(flag_ref, 1) * pairs[0])
+            store_rows(far_out, 2, 0, far_share(flag_ref, 2) * pairs[1])
+            store_rows(far_out, 2, points, far_share(flag_ref, 3) * pairs[2])
 
         @pl.loop(0, bands)
         def _(c):
@@ -617,9 +637,9 @@
         @pl.when(second)
         def _():
             pl.semaphore_wait(drained, 1)
-            start_all(far_pair_03(0, 0))
-            start_all(far_pair_02(0, 0))
-            start_all(far_pair_01(0, 0))
+            start_all(far_pair_03(2, 0))
+            start_all(far_pair_02(2, 0))
+            start_all(far_pair_01(2, 0))
 
     @pl.when(z == 1)
     def _():
@@ -627,23 +647,28 @@
 
         @pl.when(second)
         def _():
-            swap(0).start()
-
-        def band(c):
+            swap(2).start()
+
+        def band(turn):
+            c = turn + m * lax.div(turn, 2)
             clear(sums_a)
 
             def step(q):
                 s = c * groups + q
-                i = s - groups * m
-
-                @pl.when(i + EARLY < 3 * groups)
+                i = turn * groups + q
+
+                @pl.when((i < CATCH_UP) & (lax.rem(i, 2) == 0))
                 def _():
-                    relay(i + EARLY)
+                    relay(EARLY + lax.div(i, 2))
+
+                @pl.when((i >= CATCH_UP) & (i + EARLY - CATCH_UP // 2 < 3 * groups))
+                def _():
+                    relay(i + EARLY - CATCH_UP // 2)
 
                 one[...] = transform(white0, s)
                 cross_into(sums_a, one, spec.at[s])
 
-                @pl.when(first & (c == bands - 2))
+                @pl.when(first & (turn == bands - 2))
                 def _():
                     late = (bands - 1) * groups + q
                     arrived(2, late)
@@ -658,7 +683,7 @@
             add_piece(c, channels, far_share(zero_flags, 1) * piece)
             swap(c).start()
 
-        over_bands(m, m + bands - 1, band)
+        over_bands(0, bands - 1, band)
 
         @pl.when(first)
         def _():
@@ -694,26 +719,26 @@
 
         @pl.when(second)
         def _():
-            swap(0).start()
+            swap(2).start()
 
         clear(sums_a)
 
         def early_step(q):
-            s = m * groups + q
-            arrived(0, s)
-            pass_on(s, 2, 3).start()
-            one[...] = transform(white0, s)
-            cross_into(sums_a, one, spec.at[s])
+            arrived(0, q)
+            pass_on(q, 2, 3).start()
+            one[...] = transform(white0, q)
+            cross_into(sums_a, one, spec.at[q])
 
         over_windows(early_step)
         piece = lags_of(sums_a[...], 2 * points)
-        store_rows(near_out, m, 0, near_share(zero_flags, 2) * piece)
-        near_out[m, :, points : points + channels] = jnp.zeros((2, channels, BAND), near_out.dtype)
-        start_all(near_from_2(m))
-        add_piece(m, 2 * channels, far_share(zero_flags, 2) * piece)
-        swap(m).start()
-
-        def band(c):
+        store_rows(near_out, 0, 0, near_share(zero_flags, 2) * piece)
+        near_out[0, :, points : points + channels] = jnp.zeros((2, channels, BAND), near_out.dtype)
+        start_all(near_from_2(0))
+        add_piece(0, 2 * channels, far_share(zero_flags, 2) * piece)
+        swap(0).start()
+
+        def band(turn):
+            c = turn + m * lax.div(turn, 2)
             clear(sums_a, sums_b, sums_c)
 
             def step(q):
@@ -743,16 +768,16 @@
             add_piece(c, channels, near_share(flag_ref, 1) * ahead)
             swap(c).start()
 
-        over_bands(1 + m, bands - 1 + m, band)
+        over_bands(1, bands - 1, band)
 
     @pl.when(z == 3)
     def _():
         flags_to(0, 3, 0).wait_recv()
         flags_to(1, 3, 0).wait_recv()
 
-        @pl.loop(1 + m, bands - 1 + m)
-        def _(c):
-            swap(c).start()
+        @pl.loop(1, bands - 1)
+        def _(turn):
+            swap(turn + m * lax.div(turn, 2)).start()
 
         def band(c):
             clear(sums_a)
@@ -769,7 +794,7 @@
             start_all(near_pair_23(c))
             add_piece(c, channels, far_share(two_flags, 1) * piece)
 
-            @pl.when(c == m)
+            @pl.when(c == 0)
             def _():
                 clear(sums_c)
 
@@ -787,7 +812,7 @@
 
             swap(c).start()
 
-        over_bands(0, 2, lambda i: band(i * (bands - 1 - (bands - 2) * m)))
+        over_bands(0, 2, lambda turn: band(turn * (bands - 1 - m)))
 
     def lanes_of(core, c):
         return pl.ds(pl.multiple_of(core * half + place(c) * BAND, BAND), BAND)
@@ -809,32 +834,32 @@
 
     def take_at_0(target):
         for sender in range(halves):
-            def band(c):
+            def band(turn):
+                c = turn + sender * lax.div(turn, 2)
                 take(target, c, 1, sender, channels, one_pair)
                 take(target, c, 2, sender, 2 * channels, three_pairs)
 
-            over_bands(sender, sender + bands - 1, band)
-            take(target, sender, 3, sender, 3 * channels, three_pairs)
+            over_bands(0, bands - 1, band)
+            take(target, 0, 3, sender, 3 * channels, three_pairs)
         take(target, bands - 1, 1, 0, channels, three_pairs)
 
     def take_at_1(target):
-        take(target, 0, 0, 1, channels, one_pair)
+        take(target, 2, 0, 1, channels, one_pair)
 
     def take_at_2(target):
-        take(target, 0, 0, 1, 2 * channels, two_pairs)
-        take(target, 0, 3, 1, channels, one_pair)
-        take(target, 1, 3, 1, channels, one_pair)
-        take(target, 0, 3, 0, channels, one_pair)
-        take(target, bands - 1, 3, 0, channels, one_pair)
+        for sender in range(halves):
+            take(target, 0, 3, sender, channels, one_pair)
+            take(target, bands - 1 - sender, 3, sender, channels, one_pair)
+        take(target, 2, 0, 1, 2 * channels, two_pairs)
         take(target, bands - 1, 1, 0, 2 * channels, two_pairs)
 
     def take_at_3(target):
-        take(target, 0, 0, 1, 3 * channels, three_pairs)
         for sender in range(halves):
-            def band(c):
-                take(target, c, 2, sender, channels, three_pairs)
-
-            over_bands(1 + sender, bands - 1 + sender, band)
+            def band(turn):
+                take(target, turn + sender * lax.div(turn, 2), 2, sender, channels, three_pairs)
+
+            over_bands(1, bands - 1, band)
+        take(target, 2, 0, 1, 3 * channels, three_pairs)
         take(target, bands - 1, 1, 0, 3 * channels, three_pairs)
 
     for block, step in enumerate((take_at_0, take_at_1, take_at_2, take_at_3)):
@@ -843,9 +868,11 @@
             def _():
                 step(target)
 
-    @pl.when(sends_edge)
-    def _():
-        edge().wait_send()
+    @pl.when(at_cut)
+    def _():
+        @pl.loop(0, groups)
+        def _(q):
+            edge(q).wait_send()
 
     def sent_range(begin, end, lane):
         @pl.loop(begin, end)
@@ -856,22 +883,24 @@
     def _():
         for device in range(1, blocks):
             flags_to(0, device, device - 1).wait_send()
-        sent_range(groups * m, pieces - 1 + m, 0)
+        sent_range(0, (3 - m) * groups, 0)
+        sent_range(3 * groups, pieces - 1 + m, 0)
 
         @pl.when(second)
         def _():
-            finish_all(far_pair_01(0, 0))
-            finish_all(far_pair_02(0, 0))
-            finish_all(far_pair_03(0, 0))
+            finish_all(far_pair_01(2, 0))
+            finish_all(far_pair_02(2, 0))
+            finish_all(far_pair_03(2, 0))
 
     @pl.when(z == 1)
     def _():
-        sent_range(groups * m, groups * m + 3 * groups, 0)
-        over_bands(m, m + bands - 1, lambda c: finish_all(near_from_1(c)))
+        sent_range(0, 2 * groups, 0)
+        sent_range((2 + m) * groups, (3 + m) * groups, 0)
+        over_bands(0, bands - 1, lambda turn: finish_all(near_from_1(turn + m * lax.div(turn, 2))))
 
         @pl.when(second)
         def _():
-            sent_range(0, groups, 1)
+            sent_range(2 * groups, 3 * groups, 1)
 
         @pl.when(first)
         def _():
@@ -890,33 +919,30 @@
 
         @pl.when(second)
         def _():
-            sent_range(0, groups, 0)
-
-        sent_range(0, groups + groups * m, 1)
-        sent_range(groups * m, groups + groups * m, 2)
-        finish_all(near_from_2(m))
-
-        def band(c):
+            sent_range(2 * groups, 3 * groups, 0)
+            sent_range(2 * groups, 3 * groups, 1)
+
+        sent_range(0, groups, 1)
+        sent_range(0, groups, 2)
+        finish_all(near_from_2(0))
+
+        def band(turn):
+            c = turn + m * lax.div(turn, 2)
             finish_all(near_from_2(c))
             finish_all(far_from_2(c))
 
-        over_bands(1 + m, bands - 1 + m, band)
+        over_bands(1, bands - 1, band)
 
     @pl.when(z == 3)
     def _():
-        @pl.when(first)
-        def _():
-            sent_range(groups, pieces, 0)
-            finish_all(near_pair_23(bands - 1))
-
-        @pl.when(second)
-        def _():
-            sent_range(0, groups, 0)
-            sent_range(2 * groups, pieces, 0)
-            finish_all(near_pair_23(0))
-
-        finish_all(near_pair_23(m))
-        finish_all(near_from_3(m))
+        sent_range(groups, pieces, 0)
+        finish_all(near_pair_23(0))
+        finish_all(near_pair_23(bands - 1 - m))
+        finish_all(near_from_3(0))
+
+
+def in_hbm(array):
+    return pltpu.with_memory_space_constraint(array, pltpu.HBM)
 
 
 def four_block_shards(spectra, counts, owners):
@@ -946,9 +972,10 @@
     out = pl.pallas_call(
         stack_kernel,
         out_shape=jax.ShapeDtypeStruct((2, kept, bins), F32),
-        in_specs=[hbm, smem, smem, hbm],
+        in_specs=[hbm, smem, hbm, hbm],
         out_specs=pl.BlockSpec(memory_space=pltpu.VMEM),
         scratch_shapes=[
+            pltpu.SMEM(owners.shape, owners.dtype),
             pltpu.VMEM((2, windows, channels, half + 2 * EDGE), BF16),
             pltpu.VMEM(window.shape, BF16),
             pltpu.VMEM(forward.shape, BF16),
@@ -962,16 +989,16 @@
             shares, shares,
             pltpu.VMEM((blocks, halves, bands, 2, kept, BAND), BF16),
             pltpu.VMEM((bands, 2, kept, BAND), F32),
-            dma((groups,)), dma((3,)), dma((1,)), dma((1,)), dma((3,)), dma((2,)),
+            dma((groups,)), dma((3,)), dma((groups,)), dma((groups,)), dma((3,)), dma((2,)),
             dma((3, pieces)), dma((blocks, pieces)),
             dma((3, halves, bands)), dma((blocks, halves, bands)),
             dma((bands,)), dma((bands,)),
             pltpu.SemaphoreType.REGULAR, pltpu.SemaphoreType.REGULAR, pltpu.SemaphoreType.REGULAR,
         ],
         compiler_params=pltpu.CompilerParams(
-            collective_id=0, has_side_effects=True, vmem_limit_bytes=55000000
+            collective_id=0, has_side_effects=True, vmem_limit_bytes=40 * 1024 * 1024
         ),
-    )(spectra, counts, owners.reshape(-1), jnp.asarray(tables))
+    )(in_hbm(spectra), counts, in_hbm(owners), in_hbm(jnp.asarray(tables)))
     return out[:, None]
 
 

time: 56.9 us -> 53.9 us (0.947)
  Pallas kernels: 54.4 us -> 52.1 us
  local copies, waits for them, and re-layouts: 1.71 us -> 1.06 us
    pallas_call x1, Pallas kernels: 54.4 us -> 52.1 us  [four_block_shards(): pl.pallas_call(stack_kernel, out_shape=jax.ShapeDtypeStruct((2, kept, bin...]
    unnamed x3 -> x1, local copies, waits for them, and re-layouts: 1.71 us -> 1.06 us
where the time goes in v3:
time: 53.9 us; the launch traced here: 53.8 us
  Pallas kernels  52.1 us (97%)
  local copies, waits for them, and re-layouts  1.06 us (2%)
  between operations  0.66 us (1%)
    pallas_call x1, Pallas kernels, four_block_shards(): pl.pallas_call(stack_kernel, out_shape=jax.ShapeDtypeStruct((2, kept, bin...  52.1 us

profile of v3, /device:TPU:1, one launch (start us, length us, event | category | flops | bytes accessed | tf_op | source)
XLA Modules:
  0.0 53.8 jit_solution(11171731525865658693)
XLA Ops:
  0.7 52.1 %shard_map.46 = f32[2,160,1024]{2,1,0:T(8,128)S(1)} custom-call(bf16[2,16,64,1024]{3,2,1,0:T(8,128)(2,1)} %spectra_ref.1, s32[1]{0:T(128)S(6)} %copy.7.counts_ref, s32[1,4]{1,0:T(1,128)} %owners_hbm.1, bf16[2048,512]{1,0:T(8,128)(2,1)} %constant.2.clone.tables_ref), custom_call_target="tpu_custom_call" | custom-call | tf_op jit(solution)/shard_map/pallas_call | solution.py:972
  52.7 1.1 %copy.8 = f32[2,1,160,1024]{3,2,1,0:T(8,128)} copy(f32[2,1,160,1024]{3,2,1,0:T(8,128)S(1)} %bitcast.3) | data formatting | bytes 2621440

commit v4 on v3

--- a/solution.py
+++ b/solution.py
@@ -166,7 +166,7 @@
     white, white0, white1, white2, white3, spec, one, two, three, sums_a, sums_b, sums_c,
     stack, near_out, far_out, inbox, swapped,
     load_sem, constant_sem, edge_send, edge_recv, flag_send, flag_recv,
-    block_send, block_recv, result_send, result_recv, swap_send, swap_recv, known, spread, drained,
+    block_send, block_recv, result_send, result_recv, swap_send, swap_recv, known, spread, drained, across,
 ):
     windows, channels = x_ref.shape[1:3]
     half = x_ref.shape[3] - 2 * EDGE
@@ -326,7 +326,7 @@
     pl.semaphore_signal(barrier, inc=1, device_id=partner, device_id_type=MESH)
     at_cut = x != m
 
-    @pl.when(at_cut)
+    @pl.when(at_cut & (z > 0))
     def _():
         pl.semaphore_signal(barrier, inc=1, device_id={"bins": 1 - x, "pairs": x}, device_id_type=MESH)
 
@@ -360,7 +360,7 @@
         whiten(q, mirrored * BAND, bands - 1, lambda j: j + mirrored * (bands - 2 - 2 * j))
 
     def send_edge(q):
-        @pl.when(at_cut)
+        @pl.when(at_cut & (z > 0))
         def _():
             edge(q).start()
 
@@ -400,10 +400,15 @@
     constants[0].wait()
     load(0).wait()
     whiten(0, mirrored * (bands - 1) * BAND, 1, lambda j: 0)
-    pl.semaphore_wait(barrier, beside + 1 + jnp.where(at_cut, 1, 0))
+    pl.semaphore_wait(barrier, beside + 1 + jnp.where(at_cut & (z > 0), 1, 0))
     send_first(0)
     send_edge(0)
     tell_beside(known)
+
+    @pl.when(at_cut & (z == 1))
+    def _():
+        pl.semaphore_signal(across, inc=1, device_id={"bins": 1 - x, "pairs": x}, device_id_type=MESH)
+
     whiten(0, BAND, bands - 2, lambda j: 1 + j + mirrored * (bands - 3 - 2 * j))
     send_inner(0)
 
@@ -437,9 +442,20 @@
 
     lax.fori_loop(1, groups // 2, inner_step, 0)
     pl.semaphore_wait(known, beside)
+
+    @pl.when(at_cut & (z == 1))
+    def _():
+        pl.semaphore_wait(across, 1)
+
     tell_beside(spread)
     lax.fori_loop(groups // 2, groups, inner_step, 0)
     pl.semaphore_wait(spread, beside)
+
+    @pl.when(at_cut & (z == 0))
+    def _():
+        @pl.loop(0, groups)
+        def _(q):
+            edge(q).start()
 
     @pl.when(z == 0)
     def _():
@@ -993,7 +1009,8 @@
             dma((3, pieces)), dma((blocks, pieces)),
             dma((3, halves, bands)), dma((blocks, halves, bands)),
             dma((bands,)), dma((bands,)),
-            pltpu.SemaphoreType.REGULAR, pltpu.SemaphoreType.REGULAR, pltpu.SemaphoreType.REGULAR,
+            pltpu.SemaphoreType.REGULAR, pltpu.SemaphoreType.REGULAR,
+            pltpu.SemaphoreType.REGULAR, pltpu.SemaphoreType.REGULAR,
         ],
         compiler_params=pltpu.CompilerParams(
             collective_id=0, has_side_effects=True, vmem_limit_bytes=40 * 1024 * 1024

time: 53.9 us -> 53.2 us (0.987)
  Pallas kernels: 52.1 us -> 51.3 us
    pallas_call x1, Pallas kernels: 52.1 us -> 51.3 us  [four_block_shards(): pl.pallas_call(stack_kernel, out_shape=jax.ShapeDtypeStruct((2, kept, bin...]
where the time goes in v4:
time: 53.2 us; the launch traced here: 53 us
  Pallas kernels  51.3 us (96%)
  local copies, waits for them, and re-layouts  1.06 us (2%)
  between operations  0.66 us (1%)
    pallas_call x1, Pallas kernels, four_block_shards(): pl.pallas_call(stack_kernel, out_shape=jax.ShapeDtypeStruct((2, kept, bin...  51.3 us

profile of v4, /device:TPU:1, one launch (start us, length us, event | category | flops | bytes accessed | tf_op | source)
XLA Modules:
  0.0 53.0 jit_solution(17960689761979303848)
XLA Ops:
  0.7 51.3 %shard_map.46 = f32[2,160,1024]{2,1,0:T(8,128)S(1)} custom-call(bf16[2,16,64,1024]{3,2,1,0:T(8,128)(2,1)} %spectra_ref.1, s32[1]{0:T(128)S(6)} %copy.7.counts_ref, s32[1,4]{1,0:T(1,128)} %owners_hbm.1, bf16[2048,512]{1,0:T(8,128)(2,1)} %constant.2.clone.tables_ref), custom_call_target="tpu_custom_call" | custom-call | tf_op jit(solution)/shard_map/pallas_call | solution.py:988
  52.0 1.1 %copy.8 = f32[2,1,160,1024]{3,2,1,0:T(8,128)} copy(f32[2,1,160,1024]{3,2,1,0:T(8,128)S(1)} %bitcast.3) | data formatting | bytes 2621440

commit v5 on v4

--- a/solution.py
+++ b/solution.py
@@ -397,6 +397,12 @@
         def _(s):
             own_to(block, s, lane, device).start()
 
+    def clear_edge(begin, count):
+        @pl.when(~at_cut)
+        def _():
+            x_ref[:, begin : begin + count, :, edge_lanes(m)] = jnp.zeros((2, count, channels, EDGE), x_ref.dtype)
+
+    clear_edge(0, GROUP)
     constants[0].wait()
     load(0).wait()
     whiten(0, mirrored * (bands - 1) * BAND, 1, lambda j: 0)
@@ -427,9 +433,7 @@
     def _():
         flags_to(1, 3, 0).start()
 
-    @pl.when(~at_cut)
-    def _():
-        x_ref[:, :, :, edge_lanes(m)] = jnp.zeros((2, windows, channels, EDGE), x_ref.dtype)
+    clear_edge(GROUP, windows - GROUP)
 
     def inner_step(q, carry):
         load(q).wait()

time: 53.2 us -> 53.2 us (level)
  no operation moved by 1% of the time
where the time goes in v5:
time: 53.2 us; the launch traced here: 53 us
  Pallas kernels  51.3 us (96%)
  local copies, waits for them, and re-layouts  1.06 us (2%)
  between operations  0.66 us (1%)
    pallas_call x1, Pallas kernels, four_block_shards(): pl.pallas_call(stack_kernel, out_shape=jax.ShapeDtypeStruct((2, kept, bin...  51.3 us

profile of v5, /device:TPU:1, one launch (start us, length us, event | category | flops | bytes accessed | tf_op | source)
XLA Modules:
  0.0 53.0 jit_solution(5224737326447987888)
XLA Ops:
  0.7 51.3 %shard_map.46 = f32[2,160,1024]{2,1,0:T(8,128)S(1)} custom-call(bf16[2,16,64,1024]{3,2,1,0:T(8,128)(2,1)} %spectra_ref.1, s32[1]{0:T(128)S(6)} %copy.7.counts_ref, s32[1,4]{1,0:T(1,128)} %owners_hbm.1, bf16[2048,512]{1,0:T(8,128)(2,1)} %constant.2.clone.tables_ref), custom_call_target="tpu_custom_call" | custom-call | tf_op jit(solution)/shard_map/pallas_call | solution.py:992
  52.0 1.1 %copy.8 = f32[2,1,160,1024]{3,2,1,0:T(8,128)} copy(f32[2,1,160,1024]{3,2,1,0:T(8,128)S(1)} %bitcast.3) | data formatting | bytes 2621440

commit v6 on v5

--- a/solution.py
+++ b/solution.py
@@ -779,7 +779,8 @@
             over_windows(step)
             near, beyond = lags_of_many(sums_a, sums_c)
             store_sums(near_out, c, [near_share(zero_flags, 2) * near, near_share(zero_flags, 3) * beyond])
-            start_all(near_from_2(c))
+            for copy in reversed(near_from_2(c).values()):
+                copy.start()
             ahead = sums_b[...]
             store_rows(far_out, c, 0, far_share(flag_ref, 1) * ahead)
             store_rows(far_out, c, points, far_share(zero_flags, 3) * beyond)

time: 53.2 us -> 53.2 us (level)
  no operation moved by 1% of the time
where the time goes in v6:
time: 53.2 us; the launch traced here: 53 us
  Pallas kernels  51.3 us (96%)
  local copies, waits for them, and re-layouts  1.06 us (2%)
  between operations  0.66 us (1%)
    pallas_call x1, Pallas kernels, four_block_shards(): pl.pallas_call(stack_kernel, out_shape=jax.ShapeDtypeStruct((2, kept, bin...  51.3 us

profile of v6, /device:TPU:1, one launch (start us, length us, event | category | flops | bytes accessed | tf_op | source)
XLA Modules:
  0.0 53.0 jit_solution(18062351683422935027)
XLA Ops:
  0.7 51.3 %shard_map.46 = f32[2,160,1024]{2,1,0:T(8,128)S(1)} custom-call(bf16[2,16,64,1024]{3,2,1,0:T(8,128)(2,1)} %spectra_ref.1, s32[1]{0:T(128)S(6)} %copy.7.counts_ref, s32[1,4]{1,0:T(1,128)} %owners_hbm.1, bf16[2048,512]{1,0:T(8,128)(2,1)} %constant.2.clone.tables_ref), custom_call_target="tpu_custom_call" | custom-call | tf_op jit(solution)/shard_map/pallas_call | solution.py:993
  52.0 1.1 %copy.8 = f32[2,1,160,1024]{3,2,1,0:T(8,128)} copy(f32[2,1,160,1024]{3,2,1,0:T(8,128)S(1)} %bitcast.3) | data formatting | bytes 2621440
